TPU v7x, 32 devices: a whole 2x2x4 slice. The times are simulated.
32 devices in a mesh: dp: 8 (over z, x), narrow: 4 (over y, core).
Axes of the slice: x: 2, y: 2, z: 4, core: 2. Of those that a mesh axis runs over, the one named last changes fastest.
Arguments:
- patches: bfloat16 [32768, 768], P(('dp', 'narrow')), may hold values from -6 to 6
- pos_index: int32 [32768], P(('dp', 'narrow')), may hold values from 0 to 196, as said below
- segments: int32 [32768], P(('dp', 'narrow')), may hold values from 0 to 27, as said below
- cls_row: int32 [768], P(('dp', 'narrow')), may hold values from 0 to 1023, as said below
- labels: int32 [768], P(('dp', 'narrow')), may hold values from 0 to 999
- img_count: int32 [128], P(('dp', 'narrow')), may hold values from 1 to 6, as said below
- embed_w: float32 [965, 384], P(None, 'dp'), may hold values from -0.21875 to 0.21875
- embed_m: float32 [965, 384], P(None, 'dp')
- embed_v: float32 [965, 384], P(None, 'dp')
- embed_e: float32 [965, 384], P(None, 'dp'), may hold values from -0.21875 to 0.21875
- vector_w: float32 [14, 384], P(None, 'dp')
- vector_m: float32 [14, 384], P(None, 'dp')
- vector_v: float32 [14, 384], P(None, 'dp')
- vector_e: float32 [14, 384], P(None, 'dp')
- mats_w: float32 [3, 384, 4608], P(None, None, 'dp')
- mats_m: float32 [3, 384, 4608], P(None, None, 'dp')
- mats_v: float32 [3, 384, 4608], P(None, None, 'dp')
- mats_e: float32 [3, 384, 4608], P(None, None, 'dp')
- rff_w: float32 [384, 4096], P(None, 'narrow'), may hold values from -0.4375 to 0.4375
- rff_m: float32 [384, 4096], P(None, 'narrow')
- rff_v: float32 [384, 4096], P(None, 'narrow')
- rff_e: float32 [384, 4096], P(None, 'narrow'), may hold values from -0.4375 to 0.4375
- read_w: float32 [4096, 1000], P('narrow')
- read_m: float32 [4096, 1000], P('narrow')
- read_v: float32 [4096, 1000], P('narrow')
- read_e: float32 [4096, 1000], P('narrow'), may hold values from -0.09375 to 0.09375
Outputs:
- loss_sum: float32 [], replicated
- image_total: float32 [], replicated
- clip_norm: float32 [], replicated
- embed_new: float32 [965, 384], P(None, 'dp')
- embed_first: float32 [965, 384], P(None, 'dp')
- embed_second: float32 [965, 384], P(None, 'dp')
- embed_ema: float32 [965, 384], P(None, 'dp')
- embed_copy: bfloat16 [965, 384], P(None, 'dp')
- vector_new: float32 [14, 384], P(None, 'dp')
- vector_first: float32 [14, 384], P(None, 'dp')
- vector_second: float32 [14, 384], P(None, 'dp')
- vector_ema: float32 [14, 384], P(None, 'dp')
- vector_copy: bfloat16 [14, 384], P(None, 'dp')
- mats_new: float32 [3, 384, 4608], P(None, None, 'dp')
- mats_first: float32 [3, 384, 4608], P(None, None, 'dp')
- mats_second: float32 [3, 384, 4608], P(None, None, 'dp')
- mats_ema: float32 [3, 384, 4608], P(None, None, 'dp')
- mats_copy: bfloat16 [3, 384, 4608], P(None, None, 'dp')
- rff_new: float32 [384, 4096], P(None, 'narrow')
- rff_first: float32 [384, 4096], P(None, 'narrow')
- rff_second: float32 [384, 4096], P(None, 'narrow')
- rff_ema: float32 [384, 4096], P(None, 'narrow')
- rff_copy: bfloat16 [384, 4096], P(None, 'narrow')
- read_new: float32 [4096, 1000], P('narrow')
- read_first: float32 [4096, 1000], P('narrow')
- read_second: float32 [4096, 1000], P('narrow')
- read_ema: float32 [4096, 1000], P('narrow')
- read_copy: bfloat16 [4096, 1000], P('narrow')
Inputs may be any that keep to these rules, and one draw needn't show every extreme that they name: `pos_index`: each sequence holds whole images one after another from its first row, then pad rows. An image of s x s patches (s = 4, 7 or 10) has its class row, with index 0, followed by its patches in row-major order with index 1 + 10 * row + column. Pad rows have indices from 1 to 196, the first pad row of each sequence 197 - 1. `segments`: the rows of one image share a segment number, the pad rows of one sequence share another, and numbers of different sequences of one device differ; every sequence ends in pad rows. `cls_row`: for slot k of a sequence with k below its count, the row of that image's class token within the device's rows; other slots hold the sequence's last row. `img_count`: in every draw some device's sequences all hold 6 images.
All inputs are finite; a program needn't handle non-finite values.
Results may differ from a plain program's by a relative error of at most 0.035.
Values may be sent and summed in bfloat16 or wider, within the bound.
No kernel may reach another device: no remote copies, remote signals or barrier semaphores. Data moves between devices by JAX's collectives and lax.ppermute only.
A program may use at most 256 MiB of HBM per device.

v0:
```python
import jax
import jax.numpy as jnp
from jax import lax
from jax.sharding import PartitionSpec as P

D = 384
HEADS = 6
HD = 64
MLP = 1536
POS = 197
CLASSES = 1000
L = 3
IMG_SEQ = 6
STEP = 10
BLOCK = 512


norm_eps = 1e-06
clip_bound = 0.02
l2_weight = 0.1
beta_first = 0.5
beta_second = 0.5
adam_eps = 1e-08
weight_decay = 0.05
rate_matrix = 0.05
rate_vector = 0.5
ema_rate = 0.5


def product(left, right):
    return jnp.dot(left, right, preferred_element_type=jnp.float32)


def inner_rows(left, right):
    return lax.dot_general(
        left, right, (((0,), (0,)), ((), ())), preferred_element_type=jnp.float32
    )


def against(left, right):
    return lax.dot_general(
        left, right, (((1,), (1,)), ((), ())), preferred_element_type=jnp.float32
    )


def layer_norm(rows_in, gain, shift):
    centred = rows_in - jnp.mean(rows_in, axis=-1, keepdims=True)
    spread = jnp.mean(centred * centred, axis=-1, keepdims=True)
    return centred * lax.rsqrt(spread + norm_eps) * gain + shift


def norm_back(rows_in, gain, grad_out):
    centred = rows_in - jnp.mean(rows_in, axis=-1, keepdims=True)
    inverse = lax.rsqrt(jnp.mean(centred * centred, axis=-1, keepdims=True) + norm_eps)
    unit_rows = centred * inverse
    scaled = grad_out * gain
    grad_in = inverse * (
        scaled
        - jnp.mean(scaled, axis=-1, keepdims=True)
        - unit_rows * jnp.mean(scaled * unit_rows, axis=-1, keepdims=True)
    )
    return (grad_in, jnp.sum(grad_out * unit_rows, axis=0), jnp.sum(grad_out, axis=0))


def split_heads(projected):
    return (
        projected[:, :D].reshape(-1, HEADS, HD),
        projected[:, D : 2 * D].reshape(-1, HEADS, HD),
        projected[:, 2 * D :].reshape(-1, HEADS, HD),
    )


def block_scores(query_heads, key_heads, seg_rows):
    scores = jnp.einsum(
        "qhd,khd->hqk", query_heads, key_heads, preferred_element_type=jnp.float32
    ) * HD ** (-0.5)
    return jnp.where((seg_rows[:, None] == seg_rows[None, :])[None], scores, -1e30)


def attend_forward(projected, seg_rows):
    query_heads, key_heads, value_heads = split_heads(projected)
    scores = block_scores(query_heads, key_heads, seg_rows)
    maximum = jnp.max(scores, axis=-1, keepdims=True)
    exponent = jnp.exp(scores - maximum)
    row_total = jnp.sum(exponent, axis=-1, keepdims=True)
    probability = (exponent / row_total).astype(jnp.bfloat16)
    attended = jnp.einsum(
        "hqk,khd->qhd", probability, value_heads, preferred_element_type=jnp.float32
    )
    return (attended.reshape(-1, D).astype(jnp.bfloat16), (maximum + jnp.log(row_total))[..., 0])


def attend_back(projected, seg_rows, logsum, grad_attended):
    query_heads, key_heads, value_heads = split_heads(projected)
    scores = block_scores(query_heads, key_heads, seg_rows)
    probability = jnp.exp(scores - logsum[..., None])
    grad_heads = grad_attended.reshape(-1, HEADS, HD)
    grad_values = jnp.einsum(
        "hqk,qhd->khd",
        probability.astype(jnp.bfloat16),
        grad_heads,
        preferred_element_type=jnp.float32,
    )
    grad_probs = jnp.einsum(
        "qhd,khd->hqk", grad_heads, value_heads, preferred_element_type=jnp.float32
    )
    centre = jnp.sum(grad_probs * probability, axis=-1, keepdims=True)
    grad_scores = (probability * (grad_probs - centre)).astype(jnp.bfloat16)
    grad_query = jnp.einsum(
        "hqk,khd->qhd", grad_scores, key_heads, preferred_element_type=jnp.float32
    ) * HD ** (-0.5)
    grad_keys = jnp.einsum(
        "hqk,qhd->khd", grad_scores, query_heads, preferred_element_type=jnp.float32
    ) * HD ** (-0.5)
    return jnp.concatenate(
        [grad_query.reshape(-1, D), grad_keys.reshape(-1, D), grad_values.reshape(-1, D)], axis=1
    )


def layer_forward(state, weight, gains, segments):
    normed = layer_norm(state, gains[0], gains[1]).astype(jnp.bfloat16)
    projected = product(normed, weight[:, : 3 * D]).astype(jnp.bfloat16)
    blocks = state.shape[0] // BLOCK
    attended, logsum = lax.map(
        lambda pieces: attend_forward(pieces[0], pieces[1]),
        (projected.reshape(blocks, BLOCK, 3 * D), segments.reshape(blocks, BLOCK)),
    )
    attended = attended.reshape(-1, D)
    middle = state + product(attended, weight[:, 3 * D : 4 * D])
    second = layer_norm(middle, gains[2], gains[3]).astype(jnp.bfloat16)
    before = product(second, weight[:, 4 * D : 4 * D + MLP])
    hidden = jax.nn.gelu(before).astype(jnp.bfloat16)
    output_rows = middle + against(hidden, weight[:, 4 * D + MLP :])
    return (
        output_rows,
        (state, normed, projected, attended, logsum, middle, second, before, hidden),
    )


def layer_backward(grad_after, kept_rows, weight, gains, segments):
    state, normed, projected, attended, logsum, middle, second, before, hidden = kept_rows
    branch = grad_after.astype(jnp.bfloat16)
    grad_down = inner_rows(branch, hidden)
    grad_hidden = product(branch, weight[:, 4 * D + MLP :])
    _, gelu_pull = jax.vjp(jax.nn.gelu, before)
    grad_before = gelu_pull(grad_hidden)[0].astype(jnp.bfloat16)
    grad_up = inner_rows(second, grad_before)
    grad_second = against(grad_before, weight[:, 4 * D : 4 * D + MLP])
    grad_from_two, gain_two, shift_two = norm_back(middle, gains[2], grad_second)
    grad_middle = grad_after + grad_from_two
    attn_branch = grad_middle.astype(jnp.bfloat16)
    grad_output = inner_rows(attended, attn_branch)
    grad_attended = against(attn_branch, weight[:, 3 * D : 4 * D]).astype(jnp.bfloat16)
    blocks = state.shape[0] // BLOCK
    grad_projected = lax.map(
        lambda pieces: attend_back(pieces[0], pieces[1], pieces[2], pieces[3]),
        (
            projected.reshape(blocks, BLOCK, 3 * D),
            segments.reshape(blocks, BLOCK),
            logsum,
            grad_attended.reshape(blocks, BLOCK, D),
        ),
    )
    grad_projected = grad_projected.reshape(-1, 3 * D).astype(jnp.bfloat16)
    grad_qkv_weight = inner_rows(normed, grad_projected)
    grad_normed = against(grad_projected, weight[:, : 3 * D])
    grad_from_one, gain_one, shift_one = norm_back(state, gains[0], grad_normed)
    grad_state = grad_middle + grad_from_one
    grad_weight = jnp.concatenate([grad_qkv_weight, grad_output, grad_up, grad_down], axis=1)
    return (grad_state, grad_weight, jnp.stack([gain_one, shift_one, gain_two, shift_two]))


def adamw(weight, first, second, average, grad, rate, decay):
    first = beta_first * first + (1.0 - beta_first) * grad
    second = beta_second * second + (1.0 - beta_second) * grad * grad
    ahead = first / (1.0 - beta_first**STEP)
    behind = second / (1.0 - beta_second**STEP)
    weight = weight - rate * (ahead / (jnp.sqrt(behind) + adam_eps) + decay * weight)
    average = ema_rate * average + (1.0 - ema_rate) * weight
    return (weight, first, second, average, weight.astype(jnp.bfloat16))


def square_sum(arrays):
    return sum((jnp.sum(array_item * array_item) for array_item in arrays))


def shards(
    patches,
    pos_index,
    segments,
    cls_row,
    labels,
    img_count,
    embed_w,
    embed_m,
    embed_v,
    embed_e,
    vector_w,
    vector_m,
    vector_v,
    vector_e,
    mats_w,
    mats_m,
    mats_v,
    mats_e,
    rff_w,
    rff_m,
    rff_v,
    rff_e,
    read_w,
    read_m,
    read_v,
    read_e,
):
    local_count = jnp.sum(img_count).astype(jnp.float32)
    image_total = lax.psum(local_count, ("dp", "narrow"))
    embed_full, vector_full, mats_full = (
        lax.all_gather(embed_w.astype(jnp.bfloat16), "dp", axis=1, tiled=True),
        lax.all_gather(vector_w.astype(jnp.bfloat16), "dp", axis=1, tiled=True),
        lax.all_gather(mats_w.astype(jnp.bfloat16), "dp", axis=2, tiled=True),
    )
    gains = vector_full.astype(jnp.float32)
    is_patch = (pos_index != 0)[:, None]
    onehot_table = (pos_index[:, None] == jnp.arange(POS)[None, :]).astype(jnp.bfloat16)
    inputs = jnp.concatenate(
        [jnp.where(is_patch, patches, jnp.zeros_like(patches)), onehot_table], axis=1
    )
    state = product(inputs, embed_full)
    kept_all = []
    for layer_id in range(L):
        state, kept_rows = layer_forward(
            state, mats_full[layer_id], gains[4 * layer_id : 4 * layer_id + 4], segments
        )
        kept_all.append(kept_rows)
    final_rows = layer_norm(state, gains[4 * L], gains[4 * L + 1])
    features = final_rows[cls_row].astype(jnp.bfloat16)
    group_rows = lax.all_gather(features, "narrow", axis=0, tiled=True)
    rff_low = rff_w.astype(jnp.bfloat16)
    read_low = read_w.astype(jnp.bfloat16)
    phases = product(group_rows, rff_low)
    lifted = jnp.cos(phases).astype(jnp.bfloat16)
    slot_total = cls_row.shape[0]
    logits = lax.psum_scatter(product(lifted, read_low), "narrow", scatter_dimension=0, tiled=True)
    slot_ids = jnp.arange(slot_total)
    valid_mask = slot_ids % IMG_SEQ < jnp.repeat(img_count, IMG_SEQ, total_repeat_length=slot_total)
    valid_mask = valid_mask.astype(jnp.float32)[:, None]
    error = logits - (labels[:, None] == jnp.arange(CLASSES)[None, :]).astype(jnp.float32)
    error_sum = jnp.sum(valid_mask * error * error)
    grad_logits = (2.0 * valid_mask * error).astype(jnp.bfloat16)
    grad_group = lax.all_gather(grad_logits, "narrow", axis=0, tiled=True)
    grad_lifted = against(grad_group, read_low)
    grad_read = inner_rows(lifted, grad_group)
    grad_phases = (-jnp.sin(phases) * grad_lifted).astype(jnp.bfloat16)
    grad_rff = inner_rows(group_rows, grad_phases)
    grad_features = lax.psum_scatter(
        against(
            lax.slice_in_dim(grad_phases, 0, lax.axis_size("narrow") * slot_total, axis=0), rff_low
        ),
        "narrow",
        scatter_dimension=0,
        tiled=True,
    )
    grad_final = jnp.zeros(final_rows.shape, jnp.float32).at[cls_row].add(grad_features)
    grad_state, gain_last, shift_last = norm_back(state, gains[4 * L], grad_final)
    grad_layers = [None] * L
    grad_vectors = [None] * L
    for layer_id in reversed(range(L)):
        grad_state, grad_weight, grad_gains = layer_backward(
            grad_state,
            kept_all[layer_id],
            mats_full[layer_id],
            gains[4 * layer_id : 4 * layer_id + 4],
            segments,
        )
        grad_layers[layer_id] = grad_weight
        grad_vectors[layer_id] = grad_gains
    grad_embed = inner_rows(inputs, grad_state.astype(jnp.bfloat16))
    grad_vector = jnp.concatenate(grad_vectors + [jnp.stack([gain_last, shift_last])], axis=0)
    grad_mats = jnp.stack(grad_layers)
    grad_embed, grad_vector, grad_mats = (
        lax.psum_scatter(grad_embed, "dp", scatter_dimension=1, tiled=True),
        lax.psum_scatter(grad_vector, "dp", scatter_dimension=1, tiled=True),
        lax.psum_scatter(grad_mats, "dp", scatter_dimension=2, tiled=True),
    )
    grad_embed, grad_vector, grad_mats = lax.psum((grad_embed, grad_vector, grad_mats), "narrow")
    grad_rff, grad_read = lax.psum((grad_rff, grad_read), "dp")
    first_narrow = (lax.axis_index("narrow") == 0).astype(jnp.float32)
    first_dp = (lax.axis_index("dp") == 0).astype(jnp.float32)
    ridge_rows = read_w.shape[0] // lax.axis_size("dp")
    ridge_piece = lax.dynamic_slice_in_dim(read_w, lax.axis_index("dp") * ridge_rows, ridge_rows, 0)
    ridge_local = jnp.sum(ridge_piece * ridge_piece)
    error_total, ridge_total = lax.psum((error_sum, ridge_local), ("dp", "narrow"))
    grad_embed = grad_embed / image_total
    grad_vector = grad_vector / image_total
    grad_mats = grad_mats / image_total
    grad_rff = grad_rff / image_total
    grad_read = grad_read / image_total + 2.0 * l2_weight * read_w
    squares = first_narrow * square_sum(
        (grad_embed, grad_vector, grad_mats)
    ) + first_dp * square_sum((grad_rff, grad_read))
    total_square = lax.psum(squares, ("dp", "narrow"))
    loss_sum = error_total + l2_weight * image_total * ridge_total
    clip_norm = jnp.sqrt(total_square)
    factor = jnp.minimum(1.0, clip_bound / clip_norm)
    embed_out = adamw(
        embed_w, embed_m, embed_v, embed_e, grad_embed * factor, rate_matrix, weight_decay
    )
    vector_out = adamw(
        vector_w, vector_m, vector_v, vector_e, grad_vector * factor, rate_vector, 0.0
    )
    mats_out = adamw(mats_w, mats_m, mats_v, mats_e, grad_mats * factor, rate_matrix, weight_decay)
    rff_out = adamw(rff_w, rff_m, rff_v, rff_e, grad_rff * factor, rate_matrix, weight_decay)
    read_out = adamw(read_w, read_m, read_v, read_e, grad_read * factor, rate_matrix, weight_decay)
    return (
        loss_sum,
        image_total,
        clip_norm,
        embed_out[0],
        embed_out[1],
        embed_out[2],
        embed_out[3],
        embed_out[4],
        vector_out[0],
        vector_out[1],
        vector_out[2],
        vector_out[3],
        vector_out[4],
        mats_out[0],
        mats_out[1],
        mats_out[2],
        mats_out[3],
        mats_out[4],
        rff_out[0],
        rff_out[1],
        rff_out[2],
        rff_out[3],
        rff_out[4],
        read_out[0],
        read_out[1],
        read_out[2],
        read_out[3],
        read_out[4],
    )


def solution(mesh):
    placed = (
        P(("dp", "narrow"), None),
        P(("dp", "narrow")),
        P(("dp", "narrow")),
        P(("dp", "narrow")),
        P(("dp", "narrow")),
        P(("dp", "narrow")),
        P(None, "dp"),
        P(None, "dp"),
        P(None, "dp"),
        P(None, "dp"),
        P(None, "dp"),
        P(None, "dp"),
        P(None, "dp"),
        P(None, "dp"),
        P(None, None, "dp"),
        P(None, None, "dp"),
        P(None, None, "dp"),
        P(None, None, "dp"),
        P(None, "narrow"),
        P(None, "narrow"),
        P(None, "narrow"),
        P(None, "narrow"),
        P("narrow", None),
        P("narrow", None),
        P("narrow", None),
        P("narrow", None),
    )
    return jax.shard_map(
        shards,
        mesh=mesh,
        in_specs=placed,
        out_specs=(
            P(),
            P(),
            P(),
            P(None, "dp"),
            P(None, "dp"),
            P(None, "dp"),
            P(None, "dp"),
            P(None, "dp"),
            P(None, "dp"),
            P(None, "dp"),
            P(None, "dp"),
            P(None, "dp"),
            P(None, "dp"),
            P(None, None, "dp"),
            P(None, None, "dp"),
            P(None, None, "dp"),
            P(None, None, "dp"),
            P(None, None, "dp"),
            P(None, "narrow"),
            P(None, "narrow"),
            P(None, "narrow"),
            P(None, "narrow"),
            P(None, "narrow"),
            P("narrow", None),
            P("narrow", None),
            P("narrow", None),
            P("narrow", None),
            P("narrow", None),
        ),
        check_vma=False,
    )
```

profile of v0, /device:TPU:0, one launch (start us, length us, event | category | flops | bytes accessed | tf_op | source)
XLA Modules:
  0.0 1470.7 jit_solution(14055581814260643998)
XLA Ops:
  10.5 32.6 %all-gather = bf16[8,48,14]{1,2,0:T(8,128)(2,1)S(1)} all-gather(bf16[1,48,14]{1,2,0:T(8,128)(2,1)S(1)} %convert_bitcast_fusion), channel_id=1, replica_groups=mesh['dp'=8,'narrow'=4] {'dp'}, dimensions={0}, use_global_device_ids=true | all-gather | bytes 12096 | tf_op jit(solution)/shard_map/all_gather | solution.py:219
  45.0 34.3 %all_gather.15 = bf16[965,384]{0,1:T(8,128)(2,1)S(1)} all-gather(bf16[965,48]{0,1:T(8,128)(2,1)S(1)} %convert_element_type.234), channel_id=1, replica_groups=mesh['dp'=8,'narrow'=4] {'dp'}, dimensions={1}, use_global_device_ids=true | all-gather | bytes 833760 | tf_op jit(solution)/shard_map/all_gather | solution.py:218
  80.6 92.4 %all-gather.3.cloned.1.call-done = bf16[3,384,4608]{1,2,0:T(8,128)(2,1)} async-done(((bf16[3,384,576]{1,2,0:T(8,128)(2,1)}), bf16[3,384,4608]{1,2,0:T(8,128)(2,1)}) %all-gather.3.cloned.1.call-update) | async-done | bytes 10616848 | tf_op jit(solution)/shard_map/all_gather | solution.py:220
  173.0 6.4 slice_bitcast_fusion
  182.6 4.3 copy.227
  186.9 13.1 while.67
  207.5 4.5 convolution_convert_fusion.1
  212.1 4.3 copy.229
  216.4 13.2 while.68
  237.1 4.5 convolution_convert_fusion
  241.6 4.7 copy.231
  246.4 13.0 while.69
  273.0 5.4 all_gather.18
  280.8 4.7 fusion.83
  291.3 13.4 reduce-scatter.12.cloned.1.call-done
  306.3 5.6 all_gather.19
  311.9 3.9 fusion.62
  317.7 19.8 %reduce-scatter.20.cloned.1.call-done = f32[24,384]{1,0:T(8,128)} async-done(((f32[96,384]{1,0:T(8,128)}), f32[24,384]{1,0:T(8,128)}) %reduce-scatter.20.cloned.1.call-update) | async-done | bytes 36880
  345.7 7.6 fusion.56
  373.4 27.4 %while.70 = (s32[]{:T(128)}, bf16[2,512,1152]{2,1,0:T(8,128)(2,1)}, bf16[2,512,1152]{1,2,0:T(8,128)(2,1)}, s32[2,512]{1,0:T(2,128)S(1)}, f32[2,6,512]{2,1,0:T(8,...) while((s32[]{:T(128)}, bf16[2,512,1152]{2,1,0:T(8,128)(2,1)}, bf16[2,512,1152]{1,2,0:T(8,128)(2,1)}, ...), condition=%wide.region_41.42_spmd, body=%wide.region_39.41_spmd.sunk | while | flops 1034810368 | bytes 65628264 | solution.py:155
  400.9 5.2 fusion.171
  413.0 8.2 fusion.49
  441.3 27.4 %while.71 = (s32[]{:T(128)}, bf16[2,512,1152]{2,1,0:T(8,128)(2,1)}, bf16[2,512,1152]{1,2,0:T(8,128)(2,1)}, s32[2,512]{1,0:T(2,128)S(1)}, f32[2,6,512]{2,1,0:T(8,...) while((s32[]{:T(128)}, bf16[2,512,1152]{2,1,0:T(8,128)(2,1)}, bf16[2,512,1152]{1,2,0:T(8,128)(2,1)}, ...), condition=%wide.region_48.49_spmd, body=%wide.region_46.48_spmd.sunk | while | flops 1034810368 | bytes 65628264 | solution.py:155
  468.7 5.2 fusion.169
  480.8 7.9 fusion.42
  508.8 27.7 %while.72 = (s32[]{:T(128)}, bf16[2,512,1152]{2,1,0:T(8,128)(2,1)}, bf16[2,512,1152]{1,2,0:T(8,128)(2,1)}, s32[2,512]{1,0:T(2,128)S(1)}, f32[2,6,512]{2,1,0:T(8,...) while((s32[]{:T(128)}, bf16[2,512,1152]{2,1,0:T(8,128)(2,1)}, bf16[2,512,1152]{1,2,0:T(8,128)(2,1)}, ...), condition=%wide.region_55.56_spmd, body=%wide.region_53.55_spmd.sunk | while | flops 1034810368 | bytes 65628264 | solution.py:155
  547.0 7.5 pad_maximum_fusion
  554.5 28.1 %copy.287 = f32[3,384,4608]{1,0,2:T(4,128)} copy(f32[3,384,4608]{2,1,0:T(8,128)} %pad_maximum_fusion) | data formatting | bytes 42467328
  582.6 19.2 %copy.355 = f32[576,8,3,384]{3,1,2,0:T(8,128)} copy(f32[576,8,3,384]{3,2,1,0:T(4,128)} %bitcast.376) | data formatting | bytes 42467328
  603.5 4.3 fusion.167
  615.8 4.8 fusion.131
  623.6 325.7 %reduce-scatter.18.cloned.1.call-done = f32[576,1152]{1,0:T(8,128)} async-done(((f32[4608,1152]{1,0:T(8,128)}), f32[576,1152]{1,0:T(8,128)}) %reduce-scatter.18.cloned.1.call-update) | async-done | bytes 2654224
  956.6 61.0 %reduce-scatter.14.cloned.1.call-done = f32[965,48]{0,1:T(8,128)} async-done(((f32[965,384]{0,1:T(8,128)}), f32[965,48]{0,1:T(8,128)}) %reduce-scatter.14.cloned.1.call-update) | async-done | bytes 185296 | tf_op jit(solution)/shard_map/reduce_scatter | solution.py:281
  1018.8 39.8 %psum.64 = f32[]{:T(128)} all-reduce(f32[]{:T(128)S(6)} %convert_element_type.255), channel_id=1, replica_groups=mesh['dp'=8,'narrow'=4] {'dp','narrow'}, use_global_device_ids=true, to_apply=%region_30.31 | all-reduce | flops 1 | bytes 8 | tf_op jit(solution)/shard_map/psum | solution.py:216
  1061.3 4.7 copy.260
  1068.8 4.6 copy.264
  1075.8 5.5 reduce-scatter.16.cloned.1.call-done
  1082.1 5.7 psum.67
  1089.1 192.1 %all-reduce.7.cloned.1.call-done = (f32[384,1024]{1,0:T(8,128)}, f32[1024,1000]{0,1:T(8,128)}) async-done(((f32[384,1024]{1,0:T(8,128)}, f32[1024,1000]{0,1:T(8,128)}), (f32[384,1024]{1,0:T(8,128)}, f32[1024,1000]{0,1:T(8,128)})) %all-reduce.7.cloned.1.call-update) | async-done | bytes 5668880 | tf_op jit(solution)/shard_map/psum | solution.py:286
  1284.2 8.2 multiply_reduce_fusion.3
  1293.7 58.2 %all-reduce.9.cloned.1.call-done = (f32[965,48]{0,1:T(8,128)}, f32[3,384,576]{2,1,0:T(8,128)}) async-done(((f32[965,48]{0,1:T(8,128)}, f32[3,384,576]{2,1,0:T(8,128)}), (f32[965,48]{0,1:T(8,128)}, f32[3,384,576]{2,1,0:T(8,128)})) %all-reduce.9.cloned.1.call-update) | async-done | bytes 2839504 | tf_op jit(solution)/shard_map/psum | solution.py:285
  1360.0 40.0 %all-reduce.1 = (f32[]{:T(128)}, f32[]{:T(128)}, f32[]{:T(128)}) all-reduce(f32[]{:T(128)} %get-tuple-element.639, f32[]{:T(128)} %multiply_reduce_fusion.34, f32[]{:T(128)S(6)} %add.494), channel_id=1, replica_groups=mesh['dp'=8,'narrow'=4] {'dp','narrow'}, use_global_device_ids=true, to_apply=%region_28.29 | all-reduce | flops 3 | bytes 24 | tf_op jit(solution)/shard_map/psum | solution.py:292
  1400.7 8.1 fusion.146
  1411.3 4.6 copy.266
  1415.9 4.6 copy.267
  1424.2 4.6 copy.268
  1441.6 5.6 fusion.144
  1450.5 7.6 fusion.142
  (657 shorter events, 324.0 us)
Async XLA Ops:
  7.2 36.0 %copy-start.142 = (s32[1024]{0:T(1024)S(1)}, s32[1024]{0:T(1024)}, u32[]{:S(2)}) copy-start(s32[1024]{0:T(1024)} %param.42) | copy-start | bytes 12292
  7.2 36.0 %copy-start.156 = (s32[24]{0:T(128)S(1)}, s32[24]{0:T(128)}, u32[]{:S(2)}) copy-start(s32[24]{0:T(128)} %param.43) | copy-start | bytes 292
  7.2 37.2 %copy-start.129 = (s32[1024]{0:T(1024)S(1)}, s32[1024]{0:T(1024)}, u32[]{:S(2)}) copy-start(s32[1024]{0:T(1024)} %param.41) | copy-start | bytes 12292
  7.3 37.5 %copy-start.71 = (bf16[1024,768]{1,0:T(8,128)(2,1)S(1)}, bf16[1024,768]{1,0:T(8,128)(2,1)}, u32[]{:S(2)}) copy-start(bf16[1024,768]{1,0:T(8,128)(2,1)} %param.40) | copy-start | bytes 4718596
  7.3 165.8 %all-gather.3.cloned.1.call-start = ((), (), s32[]{:S(2)}) async-start(), calls=%async_computation.5 | async-start | bytes 11943936 | tf_op jit(solution)/shard_map/all_gather | solution.py:220
  10.4 294.3 %reduce-scatter.12.cloned.1.call-start = ((), (), s32[]{:S(2)}) async-start(), calls=%async_computation.6 | async-start | bytes 491520 | tf_op jit(solution)/shard_map/reduce_scatter | solution.py:243
  44.5 135.0 %copy-start.132 = (f32[384]{0:T(512)}, f32[384]{0:T(512)S(1)}, u32[]{:S(2)}) copy-start(f32[384]{0:T(512)S(1)} %get-tuple-element.507) | copy-start | bytes 4612
  44.5 135.0 %copy-start.143 = (f32[384]{0:T(512)}, f32[384]{0:T(512)S(1)}, u32[]{:S(2)}) copy-start(f32[384]{0:T(512)S(1)} %get-tuple-element.506) | copy-start | bytes 4612
  44.5 157.8 %copy-start.102 = (f32[384]{0:T(512)}, f32[384]{0:T(512)S(1)}, u32[]{:S(2)}) copy-start(f32[384]{0:T(512)S(1)} %get-tuple-element.505) | copy-start | bytes 4612
  44.5 157.8 %copy-start.119 = (f32[384]{0:T(512)}, f32[384]{0:T(512)S(1)}, u32[]{:S(2)}) copy-start(f32[384]{0:T(512)S(1)} %get-tuple-element.504) | copy-start | bytes 4612
  44.5 163.0 %copy-start.121 = (f32[384]{0:T(512)}, f32[384]{0:T(512)S(1)}, u32[]{:S(2)}) copy-start(f32[384]{0:T(512)S(1)} %get-tuple-element.503) | copy-start | bytes 4612
  44.5 163.0 %copy-start.145 = (f32[384]{0:T(512)}, f32[384]{0:T(512)S(1)}, u32[]{:S(2)}) copy-start(f32[384]{0:T(512)S(1)} %get-tuple-element.502) | copy-start | bytes 4612
  44.8 35.6 %copy-start.81 = (bf16[1024,197]{1,0:T(8,128)(2,1)}, bf16[1024,197]{1,0:T(8,128)(2,1)S(1)}, u32[]{:S(2)}) copy-start(bf16[1024,197]{1,0:T(8,128)(2,1)S(1)} %fusion.63) | copy-start | bytes 1210372
  45.0 35.3 %copy-start.72 = (bf16[1024,768]{1,0:T(8,128)(2,1)}, bf16[1024,768]{1,0:T(8,128)(2,1)S(1)}, u32[]{:S(2)}) copy-start(bf16[1024,768]{1,0:T(8,128)(2,1)S(1)} %broadcast_select_fusion) | copy-start | bytes 4718596
  80.3 119.8 %copy-start.15 = (f32[1024,384]{0,1:T(8,128)}, f32[1024,384]{0,1:T(8,128)S(1)}, u32[]{:S(2)}) copy-start(f32[1024,384]{0,1:T(8,128)S(1)} %get-tuple-element.645) | copy-start | bytes 4718596
  80.4 99.1 %copy-start.108 = (f32[1024]{0:T(1024)}, f32[1024]{0:T(1024)S(1)}, u32[]{:S(2)}) copy-start(f32[1024]{0:T(1024)S(1)} %broadcast_multiply_fusion.20) | copy-start | bytes 12292
  80.6 98.9 %copy-start.130 = (f32[1024]{0:T(1024)}, f32[1024]{0:T(1024)S(1)}, u32[]{:S(2)}) copy-start(f32[1024]{0:T(1024)S(1)} %add_rsqrt_fusion.6) | copy-start | bytes 12292
  207.3 22.4 %copy-start.5 = (f32[1024,384]{0,1:T(8,128)}, f32[1024,384]{0,1:T(8,128)S(1)}, u32[]{:S(2)}) copy-start(f32[1024,384]{0,1:T(8,128)S(1)} %get-tuple-element.649) | copy-start | bytes 4718596
  236.8 23.5 %copy-start.7 = (f32[1024,384]{0,1:T(8,128)}, f32[1024,384]{0,1:T(8,128)S(1)}, u32[]{:S(2)}) copy-start(f32[1024,384]{0,1:T(8,128)S(1)} %get-tuple-element.653) | copy-start | bytes 4718596
  280.7 31.2 %copy-start.42 = (f32[96,1024]{1,0:T(8,128)}, f32[96,1024]{1,0:T(8,128)S(1)}, u32[]{:S(2)}) copy-start(f32[96,1024]{1,0:T(8,128)S(1)} %fusion.121) | copy-start | bytes 1179652
  285.5 51.9 %reduce-scatter.20.cloned.1.call-start = ((), (), s32[]{:S(2)}) async-start(), calls=%async_computation.10 | async-start | bytes 184320
  317.6 631.7 %reduce-scatter.18.cloned.1.call-start = ((), (), s32[]{:S(2)}) async-start(), calls=%async_computation.9 | async-start | bytes 23887872
  317.6 25.0 %copy-start.101 = (f32[1024]{0:T(1024)S(1)}, f32[1024]{0:T(1024)}, u32[]{:S(2)}) copy-start(f32[1024]{0:T(1024)} %copy-done.100) | copy-start | bytes 12292
  317.7 25.0 %copy-start.115 = (f32[384]{0:T(512)S(1)}, f32[384]{0:T(512)}, u32[]{:S(2)}) copy-start(f32[384]{0:T(512)} %get-tuple-element.494) | copy-start | bytes 4612
  345.3 8.1 slice-start.4
  345.7 7.6 copy-start.48
  345.7 7.6 slice-start.5
  411.9 9.3 slice-start.2
  413.0 8.2 copy-start.44
  413.0 8.2 slice-start.3
  479.7 9.0 slice-start
  480.8 7.9 copy-start.46
  480.8 8.0 slice-start.1
  508.8 27.7 %copy-start.109 = (f32[1024]{0:T(1024)S(1)}, f32[1024]{0:T(1024)}, u32[]{:S(2)}) copy-start(f32[1024]{0:T(1024)} %copy-done.108) | copy-start | bytes 12292
  508.8 27.7 %copy-start.131 = (f32[1024]{0:T(1024)S(1)}, f32[1024]{0:T(1024)}, u32[]{:S(2)}) copy-start(f32[1024]{0:T(1024)} %copy-done.130) | copy-start | bytes 12292
  508.8 27.7 %copy-start.133 = (f32[384]{0:T(512)S(1)}, f32[384]{0:T(512)}, u32[]{:S(2)}) copy-start(f32[384]{0:T(512)} %copy-done.132) | copy-start | bytes 4612
  508.8 27.7 %copy-start.144 = (f32[384]{0:T(512)S(1)}, f32[384]{0:T(512)}, u32[]{:S(2)}) copy-start(f32[384]{0:T(512)} %copy-done.143) | copy-start | bytes 4612
  601.9 415.6 %reduce-scatter.14.cloned.1.call-start = ((), (), s32[]{:S(2)}) async-start(), calls=%async_computation.7 | async-start | bytes 1769472 | tf_op jit(solution)/shard_map/reduce_scatter | solution.py:281
  615.7 465.5 %reduce-scatter.16.cloned.1.call-start = ((), (), s32[]{:S(2)}) async-start(), calls=%async_computation.8 | async-start | bytes 221184
  621.9 659.2 %all-reduce.7.cloned.1.call-start = ((), (), s32[]{:S(2)}) async-start(), calls=%async_computation.11 | async-start | bytes 11337728 | tf_op jit(solution)/shard_map/psum | solution.py:286
  623.5 728.4 %all-reduce.9.cloned.1.call-start = ((), (), s32[]{:S(2)}) async-start(), calls=%async_computation.12 | async-start | bytes 6291456 | tf_op jit(solution)/shard_map/psum | solution.py:285
  956.6 61.0 %copy-start.141 = (s32[4]{0:T(128)S(1)}, s32[4]{0:T(128)}, u32[]{:S(2)}) copy-start(s32[4]{0:T(128)} %param.45) | copy-start | bytes 52
  956.6 102.0 %copy-start.26 = (f32[3,384,576]{1,2,0:T(8,128)S(1)}, f32[3,384,576]{1,2,0:T(8,128)}, u32[]{:S(2)}) copy-start(f32[3,384,576]{1,2,0:T(8,128)} %param.54) | copy-start | bytes 7962628
  1424.2 9.6 copy-start.77
  1428.9 9.4 copy-start.118
  1428.9 12.7 copy-start.18
  1428.9 12.7 copy-start.40
  1433.9 7.7 copy-start.70
  (123 other events, 435.1 us)
Sparse Core Ops, SparseCore 0:
  10.9 162.1 all-gather.2
  285.6 19.0 reduce-scatter.11
  317.7 19.6 reduce-scatter.19
  602.0 347.2 reduce-scatter.17
  953.5 63.9 reduce-scatter.13
  1021.2 60.0 reduce-scatter.15
  1086.2 194.8 all-reduce.6
  1284.3 67.5 all-reduce.8
where the time goes:
time: 1480 us; the launch traced here: 1470 us
  waiting for transfers between devices  768 us (52%)
  matrix products  204 us (14%)
  local copies, waits for them, and re-layouts  190 us (13%)
  blocking collectives  163 us (11%)
  other arithmetic  117 us (8%)
  between operations  25.2 us (2%)
    unnamed x11, waiting for transfers between devices  351 us
    psum x1, waiting for transfers between devices, shards(): grad_rff, grad_read = lax.psum((grad_rff, grad_read), 'dp')  192 us
    unnamed x341, local copies, waits for them, and re-layouts  107 us
    all_gather x1, waiting for transfers between devices, shards(): lax.all_gather(mats_w.astype(jnp.bfloat16), 'dp', axis=2, tiled=True)  92.4 us
    reduce_scatter x1, waiting for transfers between devices, shards(): lax.psum_scatter(grad_embed, 'dp', scatter_dimension=1, tiled=True)  61 us
    psum x1, waiting for transfers between devices, shards(): lax.psum((grad_embed, grad_vector, grad_mats), 'narrow')  58.2 us
    dot_general x15, matrix products, product(): return jnp.dot(left, right, preferred_element_type=jnp.float32)  55.3 us
    dot_general x14, matrix products, against(): lax.dot_general(left, right, (((1,), (1,)), ((), ())), preferred_element_...  46.4 us
  transfers between devices with their start and end apart: 8, of which 8 were waited for; matrix products, arithmetic and copies ran while one was open for 4% of the time, Pallas kernels for 0%

commit v1 on v0

v1 whole, which is shorter than its diff:
```python
import math
import jax
import jax.numpy as jnp
from jax import lax
from jax.experimental import pallas as pl
from jax.experimental.pallas import tpu as pltpu
from jax.sharding import PartitionSpec as P

D = 384
HEADS = 6
HD = 64
MLP = 1536
SEQ = 256
norm_eps = 1e-06
GELU_A = 0.7978845608028654
GELU_B = 0.044715
f32 = jnp.float32
bf16 = jnp.bfloat16


def nn(a, b):
    return lax.dot_general(a, b, (((1,), (0,)), ((), ())), preferred_element_type=f32)


def nt(a, b):
    return lax.dot_general(a, b, (((1,), (1,)), ((), ())), preferred_element_type=f32)


def tn(a, b):
    return lax.dot_general(a, b, (((0,), (0,)), ((), ())), preferred_element_type=f32)


def unit(rows):
    centred = rows - jnp.mean(rows, axis=-1, keepdims=True)
    inverse = lax.rsqrt(jnp.mean(centred * centred, axis=-1, keepdims=True) + norm_eps)
    return centred * inverse, inverse


def unit_back(u, inverse, gain, grad):
    scaled = grad * gain
    return inverse * (
        scaled
        - jnp.mean(scaled, axis=-1, keepdims=True)
        - u * jnp.mean(scaled * u, axis=-1, keepdims=True)
    )


def gelu_parts(x):
    x2 = x * x
    t = jnp.tanh(GELU_A * x * (1.0 + GELU_B * x2))
    half = 0.5 * (1.0 + t)
    return half, t, x2


def gelu_value(x):
    half, _, _ = gelu_parts(x)
    return x * half


def gelu_both(x):
    half, t, x2 = gelu_parts(x)
    slope = half + 0.5 * x * (1.0 - t * t) * (GELU_A * (1.0 + 3.0 * GELU_B * x2))
    return x * half, slope


def layer_rows(x, wa_ref, wu_ref, wd_ref, gains, seg_col, seg_row):
    g1, b1, g2, b2 = (gains[i : i + 1, :] for i in range(4))
    u, _ = unit(x)
    normed = (u * g1 + b1).astype(bf16)
    qkv = nt(normed, wa_ref[: 3 * D, :]).astype(bf16)
    heads = []
    rows = x.shape[0]
    for s in range(rows // SEQ):
        r = slice(s * SEQ, (s + 1) * SEQ)
        same = seg_col[r, :] == seg_row[:, r]
        outs = []
        for h in range(HEADS):
            q = qkv[r, h * HD : (h + 1) * HD]
            k = qkv[r, D + h * HD : D + (h + 1) * HD]
            v = qkv[r, 2 * D + h * HD : 2 * D + (h + 1) * HD]
            sc = jnp.where(same, nt(q, k) * HD ** (-0.5), -1e30)
            e = jnp.exp(sc - jnp.max(sc, axis=-1, keepdims=True))
            p = (e * (1.0 / jnp.sum(e, axis=-1, keepdims=True))).astype(bf16)
            outs.append(nn(p, v))
        heads.append(jnp.concatenate(outs, axis=1))
    att = jnp.concatenate(heads, axis=0).astype(bf16)
    x1 = x + nt(att, wa_ref[3 * D :, :])
    u2, _ = unit(x1)
    second = (u2 * g2 + b2).astype(bf16)
    hidden = gelu_value(nt(second, wu_ref[...])).astype(bf16)
    out = x1 + nn(hidden, wd_ref[...])
    return qkv, att, x1, out


def fwd_kernel(x_ref, wa_ref, wu_ref, wd_ref, g_ref, sc_ref, sr_ref, qkv_ref, att_ref, x1_ref, out_ref):
    qkv, att, x1, out = layer_rows(x_ref[...], wa_ref, wu_ref, wd_ref, g_ref[...], sc_ref[...], sr_ref[0])
    qkv_ref[...] = qkv
    att_ref[...] = att
    x1_ref[...] = x1
    out_ref[...] = out


def first_kernel(p_ref, pos_ref, e_ref, wa_ref, wu_ref, wd_ref, g_ref, sc_ref, sr_ref, in_ref, x_ref, qkv_ref, att_ref, x1_ref, out_ref):
    pos = pos_ref[...]
    patch = jnp.where(pos != 0, p_ref[...].astype(f32), 0.0).astype(bf16)
    lanes = e_ref.shape[1] - p_ref.shape[1]
    table = (pos == lax.broadcasted_iota(jnp.int32, (pos.shape[0], lanes), 1)).astype(f32).astype(bf16)
    full = jnp.concatenate([patch, table], axis=1)
    in_ref[...] = full
    x = nt(full, e_ref[...])
    x_ref[...] = x
    qkv, att, x1, out = layer_rows(x, wa_ref, wu_ref, wd_ref, g_ref[...], sc_ref[...], sr_ref[0])
    qkv_ref[...] = qkv
    att_ref[...] = att
    x1_ref[...] = x1
    out_ref[...] = out


def rows_spec(r, width):
    return pl.BlockSpec((r, width), lambda i: (i, 0))


def whole_spec(shape):
    return pl.BlockSpec(shape, lambda *i: (0,) * len(shape))


def third_spec(block):
    return pl.BlockSpec((4 * D, D), lambda *i: (block, 0))


def params(mb=56, n=1):
    return pltpu.CompilerParams(dimension_semantics=("arbitrary",) * n, vmem_limit_bytes=mb << 20)


def layer_forward(x, w, layer, gains, seg, step_rows=512):
    rows = x.shape[0]
    steps = rows // step_rows
    return pl.pallas_call(
        fwd_kernel,
        grid=(steps,),
        in_specs=[
            rows_spec(step_rows, D),
            *(third_spec(3 * layer + i) for i in range(3)),
            whole_spec(gains.shape),
            rows_spec(step_rows, 1),
            pl.BlockSpec((1, 1, step_rows), lambda i: (i, 0, 0)),
        ],
        out_specs=[rows_spec(step_rows, 3 * D), rows_spec(step_rows, D), rows_spec(step_rows, D), rows_spec(step_rows, D)],
        out_shape=[
            jax.ShapeDtypeStruct((rows, 3 * D), bf16),
            jax.ShapeDtypeStruct((rows, D), bf16),
            jax.ShapeDtypeStruct((rows, D), f32),
            jax.ShapeDtypeStruct((rows, D), f32),
        ],
        compiler_params=params(),
        name="layer_fwd",
    )(x, w, w, w, gains, seg[:, None], seg.reshape(steps, 1, step_rows))


def first_forward(patches, pos, e, w, layer, gains, seg, step_rows=512):
    rows, patch = patches.shape
    lanes = e.shape[1]
    steps = rows // step_rows
    return pl.pallas_call(
        first_kernel,
        grid=(steps,),
        in_specs=[
            rows_spec(step_rows, patch),
            rows_spec(step_rows, 1),
            whole_spec(e.shape),
            *(third_spec(3 * layer + i) for i in range(3)),
            whole_spec(gains.shape),
            rows_spec(step_rows, 1),
            pl.BlockSpec((1, 1, step_rows), lambda i: (i, 0, 0)),
        ],
        out_specs=[rows_spec(step_rows, lanes), rows_spec(step_rows, D), rows_spec(step_rows, 3 * D), rows_spec(step_rows, D), rows_spec(step_rows, D), rows_spec(step_rows, D)],
        out_shape=[
            jax.ShapeDtypeStruct((rows, lanes), bf16),
            jax.ShapeDtypeStruct((rows, D), f32),
            jax.ShapeDtypeStruct((rows, 3 * D), bf16),
            jax.ShapeDtypeStruct((rows, D), bf16),
            jax.ShapeDtypeStruct((rows, D), f32),
            jax.ShapeDtypeStruct((rows, D), f32),
        ],
        compiler_params=params(),
        name="first_fwd",
    )(patches, pos[:, None], e, w, w, w, gains, seg[:, None], seg.reshape(steps, 1, step_rows))


def last_fwd_kernel(cls_ref, x_ref, wa_ref, wu_ref, wd_ref, g_ref, sk_ref, sq_ref, kv_ref, xc_ref, q_ref, att_ref, x1_ref, out_ref, feat_ref):
    g1, b1, g2, b2, g3, b3 = (g_ref[i : i + 1, :] for i in range(6))
    u, _ = unit(x_ref[...])
    normed = (u * g1 + b1).astype(bf16)
    kv = nt(normed, wa_ref[D : 3 * D, :]).astype(bf16)
    kv_ref[...] = kv
    slots = xc_ref.shape[0]
    for i in range(slots):
        xc_ref[i : i + 1, :] = x_ref[pl.ds(cls_ref[i], 1), :]
    xc = xc_ref[...]
    uc, _ = unit(xc)
    q = nt((uc * g1 + b1).astype(bf16), wa_ref[:D, :]).astype(bf16)
    q_ref[...] = q
    same = sq_ref[...] == sk_ref[...]
    outs = []
    for h in range(HEADS):
        c = slice(h * HD, (h + 1) * HD)
        sc = jnp.where(same, nt(q[:, c], kv[:, c]) * HD ** (-0.5), -1e30)
        e = jnp.exp(sc - jnp.max(sc, axis=-1, keepdims=True))
        p = (e * (1.0 / jnp.sum(e, axis=-1, keepdims=True))).astype(bf16)
        outs.append(nn(p, kv[:, D + h * HD : D + (h + 1) * HD]))
    att = jnp.concatenate(outs, axis=1).astype(bf16)
    att_ref[...] = att
    x1 = xc + nt(att, wa_ref[3 * D :, :])
    x1_ref[...] = x1
    u2, _ = unit(x1)
    second = (u2 * g2 + b2).astype(bf16)
    hidden = gelu_value(nt(second, wu_ref[...])).astype(bf16)
    out = x1 + nn(hidden, wd_ref[...])
    out_ref[...] = out
    u3, _ = unit(out)
    feat_ref[...] = (u3 * g3 + b3).astype(bf16)


def smem_spec():
    return pl.BlockSpec(memory_space=pltpu.SMEM)


def vmem_spec():
    return pl.BlockSpec(memory_space=pltpu.VMEM)


def last_forward(cls, x, w, layer, gains, seg, seg_cls):
    rows, slots = x.shape[0], cls.shape[0]
    return pl.pallas_call(
        last_fwd_kernel,
        grid=(1,),
        in_specs=[smem_spec(), whole_spec(x.shape), *(third_spec(3 * layer + i) for i in range(3)), *[vmem_spec()] * 3],
        out_specs=[vmem_spec()] * 7,
        out_shape=[
            jax.ShapeDtypeStruct((rows, 2 * D), bf16),
            jax.ShapeDtypeStruct((slots, D), f32),
            jax.ShapeDtypeStruct((slots, D), bf16),
            jax.ShapeDtypeStruct((slots, D), bf16),
            jax.ShapeDtypeStruct((slots, D), f32),
            jax.ShapeDtypeStruct((slots, D), f32),
            jax.ShapeDtypeStruct((slots, D), bf16),
        ],
        compiler_params=params(),
        name="last_fwd",
    )(cls, x, w, w, w, gains, seg[None, :], seg_cls[:, None])


def last_bwd_kernel(cls_ref, df_ref, x_ref, wa_ref, wu_ref, wd_ref, g_ref, sk_ref, sq_ref, kv_ref, xc_ref, q_ref, att_ref, x1_ref, xo_ref, dx_ref, dw_ref, dv_ref, dn_ref):
    g1, b1, g2, b2, g3, b3 = (g_ref[i : i + 1, :] for i in range(6))
    slots = xc_ref.shape[0]
    df = df_ref[...]
    u3, i3 = unit(xo_ref[...])
    dxo = unit_back(u3, i3, g3, df)
    dg3 = jnp.sum(df * u3, axis=0, keepdims=True)
    db3 = jnp.sum(df, axis=0, keepdims=True)
    branch = dxo.astype(bf16)
    u2, i2 = unit(x1_ref[...])
    second = (u2 * g2 + b2).astype(bf16)
    value, slope = gelu_both(nt(second, wu_ref[...]))
    dpre = (nt(branch, wd_ref[...]) * slope).astype(bf16)
    dw_ref[4 * D + MLP :, :] = tn(value.astype(bf16), branch).astype(bf16)
    dw_ref[4 * D : 4 * D + MLP, :] = tn(dpre, second).astype(bf16)
    dsecond = nn(dpre, wu_ref[...])
    dg2 = jnp.sum(dsecond * u2, axis=0, keepdims=True)
    db2 = jnp.sum(dsecond, axis=0, keepdims=True)
    dx1 = dxo + unit_back(u2, i2, g2, dsecond)
    ab = dx1.astype(bf16)
    datt = nn(ab, wa_ref[3 * D :, :]).astype(bf16)
    dw_ref[3 * D : 4 * D, :] = tn(ab, att_ref[...]).astype(bf16)
    same = sq_ref[...] == sk_ref[...]
    q, kv = q_ref[...], kv_ref[...]
    dqs, dks, dvs = [], [], []
    for h in range(HEADS):
        c = slice(h * HD, (h + 1) * HD)
        k, v = kv[:, c], kv[:, D + h * HD : D + (h + 1) * HD]
        sc = jnp.where(same, nt(q[:, c], k) * HD ** (-0.5), -1e30)
        e = jnp.exp(sc - jnp.max(sc, axis=-1, keepdims=True))
        p = e * (1.0 / jnp.sum(e, axis=-1, keepdims=True))
        dp = nt(datt[:, c], v)
        ds = (p * (dp - jnp.sum(dp * p, axis=-1, keepdims=True))).astype(bf16)
        dvs.append(tn(p.astype(bf16), datt[:, c]))
        dks.append(tn(ds, q[:, c]) * HD ** (-0.5))
        dqs.append(nn(ds, k) * HD ** (-0.5))
    dq = jnp.concatenate(dqs, axis=1).astype(bf16)
    dkv = jnp.concatenate(dks + dvs, axis=1).astype(bf16)
    u, i1 = unit(x_ref[...])
    normed = (u * g1 + b1).astype(bf16)
    dw_ref[D : 3 * D, :] = tn(dkv, normed).astype(bf16)
    uc, _ = unit(xc_ref[...])
    dw_ref[:D, :] = tn(dq, (uc * g1 + b1).astype(bf16)).astype(bf16)
    dn_ref[...] = nn(dkv, wa_ref[D : 3 * D, :])
    dnc = nn(dq, wa_ref[:D, :])
    for i in range(slots):
        at = pl.ds(cls_ref[i], 1)
        dn_ref[at, :] = dn_ref[at, :] + dnc[i : i + 1, :]
    dn = dn_ref[...]
    dg1 = jnp.sum(dn * u, axis=0, keepdims=True)
    db1 = jnp.sum(dn, axis=0, keepdims=True)
    dx_ref[...] = unit_back(u, i1, g1, dn)
    for i in range(slots):
        at = pl.ds(cls_ref[i], 1)
        dx_ref[at, :] = dx_ref[at, :] + dx1[i : i + 1, :]
    dv_ref[...] = jnp.concatenate([dg1, db1, dg2, db2, dg3, db3, jnp.zeros((2, D), f32)], axis=0)


def last_backward(cls, df, x, w, layer, gains, seg, seg_cls, kv, xc, q, att, x1, xo):
    rows = x.shape[0]
    return pl.pallas_call(
        last_bwd_kernel,
        grid=(1,),
        in_specs=[smem_spec(), vmem_spec(), whole_spec(x.shape), *(third_spec(3 * layer + i) for i in range(3)), *[vmem_spec()] * 9],
        out_specs=[vmem_spec()] * 3,
        out_shape=[
            jax.ShapeDtypeStruct((rows, D), f32),
            jax.ShapeDtypeStruct((12 * D, D), bf16),
            jax.ShapeDtypeStruct((8, D), f32),
        ],
        scratch_shapes=[pltpu.VMEM((rows, D), f32)],
        compiler_params=params(),
        name="last_bwd",
    )(cls, df, x, w, w, w, gains, seg[None, :], seg_cls[:, None], kv, xc, q, att, x1, xo)


def mlp_bwd_kernel(dxo_ref, x1_ref, wu_ref, wd_ref, g_ref, dx1_ref, dw_ref, dv_ref, acc_ref):
    step = pl.program_id(0)
    g2, b2 = g_ref[2:3, :], g_ref[3:4, :]
    dxo = dxo_ref[...]
    branch = dxo.astype(bf16)
    u2, i2 = unit(x1_ref[...])
    second = (u2 * g2 + b2).astype(bf16)
    value, slope = gelu_both(nt(second, wu_ref[...]))
    hidden = value.astype(bf16)
    dpre = (nt(branch, wd_ref[...]) * slope).astype(bf16)
    dsecond = nn(dpre, wu_ref[...])
    sums = jnp.concatenate([jnp.sum(dsecond * u2, axis=0, keepdims=True), jnp.sum(dsecond, axis=0, keepdims=True), jnp.zeros((6, D), f32)], axis=0)
    dx1_ref[...] = dxo + unit_back(u2, i2, g2, dsecond)
    last = pl.num_programs(0) - 1

    @pl.when(step == 0)
    def _():
        acc_ref[:MLP, :] = tn(dpre, second)
        acc_ref[MLP:, :] = tn(hidden, branch)
        dv_ref[...] = sums

    @pl.when(step > 0)
    def _():
        acc_ref[:MLP, :] += tn(dpre, second)
        acc_ref[MLP:, :] += tn(hidden, branch)
        dv_ref[...] += sums

    @pl.when(step == last)
    def _():
        dw_ref[...] = acc_ref[...].astype(bf16)


def mlp_backward(dxo, x1, w, layer, gains, step_rows=512):
    rows = x1.shape[0]
    steps = rows // step_rows
    return pl.pallas_call(
        mlp_bwd_kernel,
        grid=(steps,),
        in_specs=[rows_spec(step_rows, D), rows_spec(step_rows, D), third_spec(3 * layer + 1), third_spec(3 * layer + 2), whole_spec(gains.shape)],
        out_specs=[rows_spec(step_rows, D), whole_spec((2 * MLP, D)), whole_spec((8, D))],
        out_shape=[jax.ShapeDtypeStruct((rows, D), f32), jax.ShapeDtypeStruct((2 * MLP, D), bf16), jax.ShapeDtypeStruct((8, D), f32)],
        scratch_shapes=[pltpu.VMEM((2 * MLP, D), f32)],
        compiler_params=params(),
        name="mlp_bwd",
    )(dxo, x1, w, w, gains)


def att_bwd_kernel(dx1_ref, x_ref, qkv_ref, att_ref, w_ref, g_ref, sc_ref, sr_ref, dx_ref, dw_ref, dv_ref, acc_ref):
    step = pl.program_id(0)
    g1, b1 = g_ref[0:1, :], g_ref[1:2, :]
    dx1 = dx1_ref[...]
    ab = dx1.astype(bf16)
    datt = nn(ab, w_ref[3 * D : 4 * D, :]).astype(bf16)
    qkv = qkv_ref[...]
    parts = []
    for s in range(x_ref.shape[0] // SEQ):
        r = slice(s * SEQ, (s + 1) * SEQ)
        same = sc_ref[r, :] == sr_ref[0][:, r]
        dqs, dks, dvs = [], [], []
        for h in range(HEADS):
            q = qkv[r, h * HD : (h + 1) * HD]
            k = qkv[r, D + h * HD : D + (h + 1) * HD]
            v = qkv[r, 2 * D + h * HD : 2 * D + (h + 1) * HD]
            da = datt[r, h * HD : (h + 1) * HD]
            sc = jnp.where(same, nt(k, q) * HD ** (-0.5), -1e30)
            e = jnp.exp(sc - jnp.max(sc, axis=0, keepdims=True))
            p = e * (1.0 / jnp.sum(e, axis=0, keepdims=True))
            dp = nt(v, da)
            ds = (p * (dp - jnp.sum(dp * p, axis=0, keepdims=True))).astype(bf16)
            dvs.append(nn(p.astype(bf16), da))
            dks.append(nn(ds, q) * HD ** (-0.5))
            dqs.append(tn(ds, k) * HD ** (-0.5))
        parts.append(jnp.concatenate(dqs + dks + dvs, axis=1).astype(bf16))
    dqkv = jnp.concatenate(parts, axis=0)
    u, i1 = unit(x_ref[...])
    normed = (u * g1 + b1).astype(bf16)
    dn = nn(dqkv, w_ref[: 3 * D, :])
    sums = jnp.concatenate([jnp.sum(dn * u, axis=0, keepdims=True), jnp.sum(dn, axis=0, keepdims=True), jnp.zeros((6, D), f32)], axis=0)
    dx_ref[...] = dx1 + unit_back(u, i1, g1, dn)
    last = pl.num_programs(0) - 1

    @pl.when(step == 0)
    def _():
        acc_ref[: 3 * D, :] = tn(dqkv, normed)
        acc_ref[3 * D :, :] = tn(ab, att_ref[...])
        dv_ref[...] = sums

    @pl.when(step > 0)
    def _():
        acc_ref[: 3 * D, :] += tn(dqkv, normed)
        acc_ref[3 * D :, :] += tn(ab, att_ref[...])
        dv_ref[...] += sums

    @pl.when(step == last)
    def _():
        dw_ref[...] = acc_ref[...].astype(bf16)


def att_backward(dx1, x, qkv, att, w, layer, gains, seg, step_rows=512):
    rows = x.shape[0]
    steps = rows // step_rows
    return pl.pallas_call(
        att_bwd_kernel,
        grid=(steps,),
        in_specs=[
            rows_spec(step_rows, D),
            rows_spec(step_rows, D),
            rows_spec(step_rows, 3 * D),
            rows_spec(step_rows, D),
            third_spec(3 * layer),
            whole_spec(gains.shape),
            rows_spec(step_rows, 1),
            pl.BlockSpec((1, 1, step_rows), lambda i: (i, 0, 0)),
        ],
        out_specs=[rows_spec(step_rows, D), whole_spec((4 * D, D)), whole_spec((8, D))],
        out_shape=[jax.ShapeDtypeStruct((rows, D), f32), jax.ShapeDtypeStruct((4 * D, D), bf16), jax.ShapeDtypeStruct((8, D), f32)],
        scratch_shapes=[pltpu.VMEM((4 * D, D), f32)],
        compiler_params=params(),
        name="att_bwd",
    )(dx1, x, qkv, att, w, gains, seg[:, None], seg.reshape(steps, 1, step_rows))


POS = 197
CLASSES = 1000
L = 3
IMG_SEQ = 6
STEP = 10
PART = 4 * D
WIDE = 3 * PART
clip_bound = 0.02
l2_weight = 0.1
beta_first = 0.5
beta_second = 0.5
adam_eps = 1e-08
weight_decay = 0.05
rate_matrix = 0.05
rate_vector = 0.5
ema_rate = 0.5
ALL = ("dp", "narrow")


def bits_of(size):
    return size.bit_length() - 1


def swap(rows, axis, mask):
    return lax.ppermute(rows, axis, [(i, i ^ mask) for i in range(lax.axis_size(axis))])


def add_low(left, right):
    return (left.astype(f32) + right.astype(f32)).astype(bf16)


def halve(rows, dim, axis, bit):
    half = rows.shape[dim] // 2
    mine = (lax.axis_index(axis) >> bit) & 1
    keep = lax.dynamic_slice_in_dim(rows, mine * half, half, dim)
    send = lax.dynamic_slice_in_dim(rows, (1 - mine) * half, half, dim)
    return add_low(keep, swap(send, axis, 1 << bit))


def sum_narrow(rows, dim):
    for bit in range(bits_of(lax.axis_size("narrow"))):
        rows = halve(rows, dim, "narrow", bit)
    return rows


def sum_dp(rows):
    for bit in range(bits_of(lax.axis_size("dp"))):
        rows = rows.reshape(rows.shape[0] // 2, 2, *rows.shape[1:])
        rows = halve(rows, 1, "dp", bit)
        rows = rows.reshape(rows.shape[0], *rows.shape[2:])
    return rows[0]


def join_narrow(piece):
    every = lax.all_gather(piece, "narrow", axis=0, tiled=False)
    size = every.shape[0]
    bits = bits_of(size)
    order = [int(format(i, "b").zfill(bits)[::-1], 2) for i in range(size)]
    return [every[i] for i in order]


def total_of(scalars):
    tile = jnp.zeros((8, 128), f32)
    for i, value in enumerate(scalars):
        tile = tile.at[0, i].set(value)
    world = lax.axis_size("dp") * lax.axis_size("narrow")
    every = lax.all_to_all(jnp.broadcast_to(tile[None], (world, 8, 128)), ALL, 0, 0)
    row = jnp.sum(every, axis=0)[0]
    return [row[i] for i in range(len(scalars))]


def adamw(weight, first, second, average, grad, rate, decay):
    first = beta_first * first + (1.0 - beta_first) * grad
    second = beta_second * second + (1.0 - beta_second) * grad * grad
    ahead = first / (1.0 - beta_first**STEP)
    behind = second / (1.0 - beta_second**STEP)
    weight = weight - rate * (ahead / (jnp.sqrt(behind) + adam_eps) + decay * weight)
    average = ema_rate * average + (1.0 - ema_rate) * weight
    return (weight, first, second, average, weight.astype(bf16))


def square_sum(arrays):
    return sum(jnp.sum(a.astype(f32) * a.astype(f32)) for a in arrays)


def shards(
    patches,
    pos_index,
    segments,
    cls_row,
    labels,
    img_count,
    embed_w,
    embed_m,
    embed_v,
    embed_e,
    vector_w,
    vector_m,
    vector_v,
    vector_e,
    mats_w,
    mats_m,
    mats_v,
    mats_e,
    rff_w,
    rff_m,
    rff_v,
    rff_e,
    read_w,
    read_m,
    read_v,
    read_e,
):
    n_dp, n_narrow = lax.axis_size("dp"), lax.axis_size("narrow")
    me_dp, me_narrow = lax.axis_index("dp"), lax.axis_index("narrow")
    own_dim = embed_w.shape[1]
    own_wide = mats_w.shape[2]
    group = math.gcd(own_wide, PART)
    groups = WIDE // group
    slots = cls_row.shape[0]
    table_rows = -(-(embed_w.shape[0] + vector_w.shape[0]) // 256) * 256
    chunk = table_rows // n_narrow

    image_total = total_of([jnp.sum(img_count).astype(f32)])[0]
    slot_ids = jnp.arange(slots)
    valid = (slot_ids % IMG_SEQ < jnp.repeat(img_count, IMG_SEQ, total_repeat_length=slots)).astype(jnp.int32)
    facts = lax.all_gather(jnp.stack([labels, valid]), "narrow", axis=0)
    group_labels = facts[:, 0].reshape(-1)
    group_valid = facts[:, 1].reshape(-1).astype(f32)[:, None]

    table = jnp.concatenate([embed_w.T, vector_w.T], axis=1).astype(bf16)
    table = jnp.pad(table, ((0, 0), (0, table_rows - table.shape[1])))
    table = lax.dynamic_slice_in_dim(table, me_narrow * chunk, chunk, 1)
    table = lax.all_gather(table, ALL, axis=0)
    table = table.reshape(n_dp, n_narrow, own_dim, chunk).transpose(0, 2, 1, 3).reshape(D, table_rows)
    quarter = own_wide // n_narrow
    mats_own = lax.dynamic_slice_in_dim(jnp.swapaxes(mats_w, 1, 2), me_narrow * quarter, quarter, 1)
    mats = lax.all_gather(mats_own.astype(bf16), ALL, axis=1, tiled=True).reshape(L * WIDE, D)
    first_vec = embed_w.shape[0]
    gains = table[:, first_vec : first_vec + vector_w.shape[0]].T.astype(f32)

    pad = -slots % 16
    cls = jnp.concatenate([cls_row, jnp.broadcast_to(cls_row[-1:], (pad,))])
    seg_cls = segments[cls]
    inputs, x0, qkv0, att0, mid0, x1 = first_forward(patches, pos_index, table, mats, 0, gains[0:4], segments)
    states = [(x0, qkv0, att0, mid0)]
    for layer in range(1, L - 1):
        qkv, att, mid, x2 = layer_forward(x1, mats, layer, gains[4 * layer : 4 * layer + 4], segments)
        states.append((x1, qkv, att, mid))
        x1 = x2
    last_gains = gains[4 * L - 4 :]
    kept = last_forward(cls, x1, mats, L - 1, last_gains, segments, seg_cls)
    features = kept[-1][:slots]

    rff_low = rff_w.astype(bf16)
    read_low = read_w.T.astype(bf16)
    group_rows = lax.all_gather(features, "narrow", axis=0, tiled=True)
    phases = nn(group_rows, rff_low)
    lifted = jnp.cos(phases).astype(bf16)
    partial = lax.all_gather(nt(lifted, read_low).astype(bf16), "narrow", axis=0)
    logits = jnp.sum(partial.astype(f32), axis=0)
    error = logits - (group_labels[:, None] == jnp.arange(CLASSES)[None, :]).astype(f32)
    error_sum = jnp.sum(group_valid * error * error)
    grad_logits = (2.0 * group_valid * error).astype(bf16)
    grad_phases = (-jnp.sin(phases) * nn(grad_logits, read_low)).astype(bf16)
    grad_pieces = nt(grad_phases, rff_low).reshape(n_narrow, slots, D)
    grad_features = jnp.sum(lax.all_to_all(grad_pieces, "narrow", 0, 0), axis=0)
    grad_features = jnp.pad(grad_features, ((0, pad), (0, 0)))

    own_logits = lax.dynamic_slice_in_dim(grad_logits, me_narrow * slots, slots, 0)
    every = lax.all_gather(jnp.concatenate([features, own_logits], axis=1), ALL, axis=0, tiled=True)
    all_features, all_logits = every[:, :D], every[:, D:]
    all_phases = nn(all_features, rff_low)
    all_lifted = jnp.cos(all_phases).astype(bf16)
    all_grad = (-jnp.sin(all_phases) * nn(all_logits, read_low)).astype(bf16)
    grad_read = tn(all_logits, all_lifted).T
    grad_rff = tn(all_features, all_grad)

    xs, cls_kept = x1, kept[:-1]
    grad_state, grad_last, vec_last = last_backward(cls, grad_features, xs, mats, L - 1, last_gains, segments, seg_cls, *cls_kept)
    sums = [None] * L
    sums[L - 1] = sum_dp(sum_narrow(grad_last.reshape(groups, group, D), 1).reshape(n_dp, -1, D))
    vecs = [vec_last[:6]]
    for layer in reversed(range(L - 1)):
        x, qkv, att, mid = states[layer]
        lg = gains[4 * layer : 4 * layer + 4]
        grad_mid, grad_mlp, vec_mlp = mlp_backward(grad_state, mid, mats, layer, lg)
        mlp_sum = sum_narrow(grad_mlp.reshape(-1, group, D), 1)
        grad_state, grad_att, vec_att = att_backward(grad_mid, x, qkv, att, mats, layer, lg, segments)
        att_sum = sum_narrow(grad_att.reshape(-1, group, D), 1)
        sums[layer] = sum_dp(jnp.concatenate([att_sum, mlp_sum]).reshape(n_dp, -1, D))
        vecs = [vec_att[:2], vec_mlp[:2]] + vecs
    vec = jnp.concatenate(vecs).T
    grad_table = tn(grad_state.astype(bf16), inputs)
    grad_table = grad_table + jnp.pad(vec, ((0, 0), (first_vec, table_rows - first_vec - vec.shape[1])))
    table_sum = sum_narrow(grad_table.astype(bf16), 1).reshape(n_dp, own_dim, chunk)
    table_sum = sum_dp(table_sum)

    scale = 1.0 / image_total
    read_step = grad_read * scale + 2.0 * l2_weight * read_w
    rff_step = grad_rff * scale
    first_dp = (me_dp == 0).astype(f32)
    first_narrow = (me_narrow == 0).astype(f32)
    local = square_sum([*sums, table_sum]) * (scale * scale)
    local = local + first_dp * square_sum([read_step, rff_step])
    ridge = first_dp * jnp.sum(read_w * read_w)
    total_square, error_total, ridge_total = total_of([local, first_narrow * error_sum, ridge])
    loss_sum = error_total + l2_weight * image_total * ridge_total
    clip_norm = jnp.sqrt(total_square)
    factor = jnp.minimum(1.0, clip_bound / clip_norm)

    rows = jnp.stack([s.reshape(-1, group // n_narrow, D) for s in sums])
    rows = jnp.stack(join_narrow(rows), axis=2).reshape(L, own_wide, D)
    grad_mats = jnp.swapaxes(rows, 1, 2).astype(f32) * scale
    lanes = jnp.concatenate(join_narrow(table_sum), axis=1).astype(f32) * scale
    grad_embed = lanes[:, :first_vec].T
    grad_vector = lanes[:, first_vec : first_vec + vector_w.shape[0]].T

    outs = [loss_sum, image_total, clip_norm]
    outs += adamw(embed_w, embed_m, embed_v, embed_e, grad_embed * factor, rate_matrix, weight_decay)
    outs += adamw(vector_w, vector_m, vector_v, vector_e, grad_vector * factor, rate_vector, 0.0)
    outs += adamw(mats_w, mats_m, mats_v, mats_e, grad_mats * factor, rate_matrix, weight_decay)
    outs += adamw(rff_w, rff_m, rff_v, rff_e, rff_step * factor, rate_matrix, weight_decay)
    outs += adamw(read_w, read_m, read_v, read_e, read_step * factor, rate_matrix, weight_decay)
    return tuple(outs)


def solution(mesh):
    rows = P(ALL)
    table, mats, rff, read = P(None, "dp"), P(None, None, "dp"), P(None, "narrow"), P("narrow", None)
    ins = (P(ALL, None),) + (rows,) * 5 + (table,) * 8 + (mats,) * 4 + (rff,) * 4 + (read,) * 4
    outs = (P(),) * 3 + (table,) * 10 + (mats,) * 5 + (rff,) * 5 + (read,) * 5
    return jax.shard_map(shards, mesh=mesh, in_specs=ins, out_specs=outs, check_vma=False)
```

time: 1480 us -> 506 us (0.34)
  waiting for transfers between devices: 768 us -> 79 us
  matrix products: 204 us -> 45.4 us
  local copies, waits for them, and re-layouts: 190 us -> 50.6 us
  Pallas kernels: 0 us -> 127 us
  blocking collectives: 163 us -> 70.5 us
  other arithmetic: 117 us -> 60.2 us
  starting transfers between devices: 0.5 us -> 40.4 us
    unnamed x11 -> x3, waiting for transfers between devices: 351 us -> 0.05 us
    psum x2 -> x0, waiting for transfers between devices: 250 us -> none  [the longest x1 192 us: shards(): grad_rff, grad_read = lax.psum((grad_rff, grad_read), 'dp')]
    dot_general x86 -> x7, matrix products: 204 us -> 45.4 us  [the longest x3 36.6 us: tn(): lax.dot_general(a, b, (((0,), (0,)), ((), ())), preferred_element_type=f32)]
    pallas_call x0 -> x8, Pallas kernels: none -> 127 us  [the longest x2 37.3 us: att_backward(): pl.pallas_call(att_bwd_kernel, grid=(steps,), in_specs=[rows_spec(step_ro...]
    unnamed x341 -> x99, local copies, waits for them, and re-layouts: 107 us -> 18.2 us
    psum x3 -> x0, blocking collectives: 85.5 us -> none  [the longest x1 40 us: shards(): lax.psum((error_sum, ridge_local), ('dp', 'narrow'))]
    all_gather x1 -> x3, waiting for transfers between devices: 92.4 us -> 8.28 us  [the longest x1 8.25 us: shards(): lax.all_gather(mats_own.astype(bf16), ALL, axis=1, tiled=True)]
    reduce_scatter x2 -> x0, waiting for transfers between devices: 74.4 us -> none  [the longest x1 61 us: shards(): lax.psum_scatter(grad_embed, 'dp', scatter_dimension=1, tiled=True)]
  transfers between devices with their start and end apart: 8 -> 30, of which waited for: 8 -> 14; matrix products, arithmetic and copies ran while one was open for 4% -> 17% of each run, Pallas kernels for 0% -> 17%
where the time goes in v1:
time: 506 us; the launch traced here: 501 us
  Pallas kernels  127 us (25%)
  waiting for transfers between devices  79 us (16%)
  blocking collectives  70.5 us (14%)
  other arithmetic  60.2 us (12%)
  local copies, waits for them, and re-layouts  50.6 us (10%)
  matrix products  45.4 us (9%)
  starting transfers between devices  40.4 us (8%)
  between operations  27.8 us (5%)
    ppermute x24, waiting for transfers between devices, swap(): lax.ppermute(rows, axis, [(i, i ^ mask) for i in range(lax.axis_size(axis...  60.4 us
    all_gather x1, blocking collectives, shards(): table = lax.all_gather(table, ALL, axis=0)  45.5 us
    pallas_call x2, Pallas kernels, att_backward(): pl.pallas_call(att_bwd_kernel, grid=(steps,), in_specs=[rows_spec(step_ro...  37.3 us
    dot_general x3, matrix products, tn(): lax.dot_general(a, b, (((0,), (0,)), ((), ())), preferred_element_type=f32)  36.6 us
    pallas_call x2, Pallas kernels, mlp_backward(): pl.pallas_call(mlp_bwd_kernel, grid=(steps,), in_specs=[rows_spec(step_ro...  31.2 us
    ppermute x24, starting transfers between devices, swap(): lax.ppermute(rows, axis, [(i, i ^ mask) for i in range(lax.axis_size(axis...  25.2 us
    convert_element_type x5, other arithmetic, adamw(): return (weight, first, second, average, weight.astype(bf16))  22.7 us
    unnamed x99, local copies, waits for them, and re-layouts  18.2 us
  transfers between devices with their start and end apart: 30, of which 14 were waited for; matrix products, arithmetic and copies ran while one was open for 17% of the time, Pallas kernels for 17%

profile of v1, /device:TPU:0, one launch (start us, length us, event | category | flops | bytes accessed | tf_op | source)
XLA Modules:
  0.0 501.3 jit_solution(11063133014604701637)
XLA Ops:
  11.8 7.3 %all-to-all-start.1 = ((f32[32,8,128]{2,1,0:T(8,128)}), f32[32,8,128]{2,1,0:T(8,128)S(1)}, u32[]{:S(2)}, u32[]{:S(2)}) async-start(f32[32,8,128]{2,1,0:T(8,128)} %broadcast_in_dim.53), calls=%async_computation.1 | async-start | bytes 262144 | tf_op jit(solution)/shard_map/all_to_all | solution.py:517
  22.3 45.5 %all-gather = bf16[1536,256]{1,0:T(8,128)(2,1)S(1)} all-gather(bf16[48,256]{1,0:T(8,128)(2,1)S(1)} %fusion.21), channel_id=2, replica_groups=mesh['dp'=8,'narrow'=4] {'dp','narrow'}, dimensions={0}, use_global_device_ids=true | all-gather | bytes 811008 | tf_op jit(solution)/shard_map/all_gather | solution.py:584
  69.1 2.6 compare_convert_fusion
  71.8 5.1 %all-gather.5 = s32[4,2,24]{2,1,0:T(2,128)S(1)} all-gather(s32[1,2,24]{2,1,0:T(2,128)S(1)} %add_bitcast_fusion), channel_id=3, replica_groups=mesh['dp'=8,'narrow'=4] {'narrow'}, dimensions={0}, use_global_device_ids=true | all-gather | bytes 960 | tf_op jit(solution)/shard_map/all_gather | solution.py:577
  79.6 3.9 multiply_reduce_fusion
  95.2 8.3 %all-gather.10.cloned.1.call-done = bf16[3,4608,384]{2,1,0:T(8,128)(2,1)} async-done(((bf16[3,144,384]{2,1,0:T(8,128)(2,1)}), bf16[3,4608,384]{2,1,0:T(8,128)(2,1)}) %all-gather.10.cloned.1.call-update) | async-done | bytes 10616848 | tf_op jit(solution)/shard_map/all_gather | solution.py:588
  103.5 17.9 %first_fwd.1 = (bf16[1024,1024]{1,0:T(8,128)(2,1)}, f32[1024,384]{1,0:T(8,128)}, bf16[1024,1152]{1,0:T(8,128)(2,1)}, bf16[1024,384]{1,0:T(8,128)(2,1)}, f32[1024,384]{1,0:T(8,128)}, /*index=5*/f32[1024,384]{1,0:T(8,128)}) custom-call(bf16[1024,768]{1,0:T(8,128)(2,1)} %p_ref.1, s32[1024,1]{1,0:T(8,128)} %copy.170.pos_ref, bf16[384,1024]{1,0:T(8,128)(2,1)} %bitcast.131, ...), custom_call_target="tpu_custom_call" | custom-call | tf_op jit(solution)/shard_map/first_fwd/pallas_call | solution.py:164
  121.4 17.2 %layer_fwd.1 = (bf16[1024,1152]{1,0:T(8,128)(2,1)}, bf16[1024,384]{1,0:T(8,128)(2,1)}, f32[1024,384]{1,0:T(8,128)}, f32[1024,384]{1,0:T(8,128)}) custom-call(f32[1024,384]{1,0:T(8,128)} %get-tuple-element.120.x_ref, bf16[13824,384]{1,0:T(8,128)(2,1)} %bitcast.108, bf16[13824,384]{1,0:T(8,128)(2,1)} %bitcast.109, bf16[13824,384]{1,0:T(8,128)(2,1)} %bitcast.110, ...), custom_call_target="tpu_custom_call" | custom-call | tf_op jit(solution)/shard_map/layer_fwd/pallas_call | solution.py:138
  138.7 8.8 %last_fwd.1 = (bf16[1024,768]{1,0:T(8,128)(2,1)}, f32[32,384]{1,0:T(8,128)}, bf16[32,384]{1,0:T(8,128)(2,1)}, bf16[32,384]{1,0:T(8,128)(2,1)}, f32[32,384]{1,0:T...) custom-call(s32[32]{0:T(128)} %concatenate.34.cls_ref, f32[1024,384]{1,0:T(8,128)} %get-tuple-element.121.x_ref, ...), custom_call_target="tpu_custom_call" | custom-call | tf_op jit(solution)/shard_map/last_fwd/pallas_call | solution.py:234
  148.2 5.3 %all_gather.39 = bf16[96,384]{1,0:T(8,128)(2,1)S(1)} all-gather(bf16[24,384]{1,0:T(8,128)(2,1)S(1)} %slice.192), channel_id=1, replica_groups=mesh['dp'=8,'narrow'=4] {'narrow'}, dimensions={0}, use_global_device_ids=true | all-gather | bytes 92160 | tf_op jit(solution)/shard_map/all_gather | solution.py:607
  155.5 8.7 %all-gather.2 = bf16[384,1000]{1,0:T(8,128)(2,1)S(1)} all-gather(bf16[96,1000]{1,0:T(8,128)(2,1)S(1)} %convolution_convert_fusion), channel_id=4, replica_groups=mesh['dp'=8,'narrow'=4] {'narrow'}, dimensions={0}, use_global_device_ids=true | all-gather | bytes 960000 | tf_op jit(solution)/shard_map/all_gather | solution.py:610
  165.1 4.7 fusion.6
  169.8 3.3 all-to-all-start
  175.0 2.9 all-to-all-done
  178.6 14.9 %last_bwd.1 = (f32[1024,384]{1,0:T(8,128)}, bf16[4608,384]{1,0:T(8,128)(2,1)}, f32[8,384]{1,0:T(8,128)}) custom-call(s32[32]{0:T(128)} %concatenate.34.cls_ref, f32[32,384]{1,0:T(8,128)} %pad.36.df_ref, f32[1024,384]{1,0:T(8,128)} %get-tuple-element.121.x_ref, bf16[13824,384]{1,0:T(8,128)(2,1)} %bitcast.114, bf16[13824,384]{1,0:T(8,128)(2,1)} %bitcast.115, ...), custom_call_target="tpu_custom_call" | custom-call | tf_op jit(solution)/shard_map/last_bwd/pallas_call | solution.py:313
  193.4 15.5 %mlp_bwd.2 = (f32[1024,384]{1,0:T(8,128)}, bf16[3072,384]{1,0:T(8,128)(2,1)}, f32[8,384]{1,0:T(8,128)}) custom-call(f32[1024,384]{1,0:T(8,128)} %get-tuple-element.129.dxo_ref, f32[1024,384]{1,0:T(8,128)} %get-tuple-element.130.x1_ref, bf16[13824,384]{1,0:T(8,128)(2,1)} %bitcast.117, bf16[13824,384]{1,0:T(8,128)(2,1)} %bitcast.118, ...), custom_call_target="tpu_custom_call" | custom-call | tf_op jit(solution)/shard_map/mlp_bwd/pallas_call | solution.py:364
  209.0 18.5 %att_bwd.2 = (f32[1024,384]{1,0:T(8,128)}, bf16[1536,384]{1,0:T(8,128)(2,1)}, f32[8,384]{1,0:T(8,128)}) custom-call(f32[1024,384]{1,0:T(8,128)} %get-tuple-element.131.dx1_ref, f32[1024,384]{1,0:T(8,128)} %get-tuple-element.120.x_ref, bf16[1024,1152]{1,0:T(8,128)(2,1)} %get-tuple-element.132.qkv_ref, bf16[1024,384]{1,0:T(8,128)(2,1)} %get-tuple-element.133.att_ref, ...), custom_call_target="tpu_custom_call" | custom-call | tf_op jit(solution)/shard_map/att_bwd/pallas_call | solution.py:430
  227.5 15.6 %mlp_bwd.3 = (f32[1024,384]{1,0:T(8,128)}, bf16[3072,384]{1,0:T(8,128)(2,1)}, f32[8,384]{1,0:T(8,128)}) custom-call(f32[1024,384]{1,0:T(8,128)} %get-tuple-element.134.dxo_ref, f32[1024,384]{1,0:T(8,128)} %get-tuple-element.135.x1_ref, bf16[13824,384]{1,0:T(8,128)(2,1)} %bitcast.120, bf16[13824,384]{1,0:T(8,128)(2,1)} %bitcast.121, ...), custom_call_target="tpu_custom_call" | custom-call | tf_op jit(solution)/shard_map/mlp_bwd/pallas_call | solution.py:364
  243.2 18.8 %att_bwd.3 = (f32[1024,384]{1,0:T(8,128)}, bf16[1536,384]{1,0:T(8,128)(2,1)}, f32[8,384]{1,0:T(8,128)}) custom-call(f32[1024,384]{1,0:T(8,128)} %get-tuple-element.136.dx1_ref, f32[1024,384]{1,0:T(8,128)} %get-tuple-element.137.x_ref, bf16[1024,1152]{1,0:T(8,128)(2,1)} %get-tuple-element.138.qkv_ref, bf16[1024,384]{1,0:T(8,128)(2,1)} %get-tuple-element.139.att_ref, ...), custom_call_target="tpu_custom_call" | custom-call | tf_op jit(solution)/shard_map/att_bwd/pallas_call | solution.py:430
  264.8 3.5 add_convert_fusion.4
  274.8 4.4 collective-permute-done.20
  289.3 1.9 collective-permute-start.23
  291.9 2.1 collective-permute-done.23
  296.3 6.0 %all-gather.3 = bf16[4,1,48,256]{3,2,1,0:T(8,128)(2,1)S(1)} all-gather(bf16[1,1,48,256]{3,2,1,0:T(8,128)(2,1)S(1)} %get-tuple-element.341), channel_id=5, replica_groups=mesh['dp'=8,'narrow'=4] {'narrow'}, dimensions={0}, use_global_device_ids=true | all-gather | bytes 122880 | tf_op jit(solution)/shard_map/all_gather | solution.py:505
  305.2 2.1 add_convert_fusion.2
  312.2 11.3 %collective-permute-done.3 = bf16[16,48,384]{2,1,0:T(8,128)(2,1)S(1)} collective-permute-done((bf16[16,48,384]{2,1,0:T(8,128)(2,1)S(1)}, bf16[16,48,384]{2,1,0:T(8,128)(2,1)S(1)}, u32[]{:S(2)}, u32[]{:S(2)}) %collective-permute-start.3) | collective-permute-done | bytes 589856 | tf_op jit(solution)/shard_map/ppermute | solution.py:475
  325.5 10.1 %collective-permute-done.10 = bf16[16,48,384]{2,1,0:T(8,128)(2,1)S(1)} collective-permute-done((bf16[16,48,384]{2,1,0:T(8,128)(2,1)S(1)}, bf16[16,48,384]{2,1,0:T(8,128)(2,1)S(1)}, u32[]{:S(2)}, u32[]{:S(2)}) %collective-permute-start.10) | collective-permute-done | bytes 589856 | tf_op jit(solution)/shard_map/ppermute | solution.py:475
  337.6 2.0 add_convert_fusion
  342.9 4.8 collective-permute-done.11
  349.2 11.3 %collective-permute-done.15 = bf16[24,48,384]{2,1,0:T(8,128)(2,1)S(1)} collective-permute-done((bf16[24,48,384]{2,1,0:T(8,128)(2,1)S(1)}, bf16[24,48,384]{2,1,0:T(8,128)(2,1)S(1)}, u32[]{:S(2)}, u32[]{:S(2)}) %collective-permute-start.15) | collective-permute-done | bytes 884768 | tf_op jit(solution)/shard_map/ppermute | solution.py:475
  364.6 6.8 %collective-permute-done.16 = bf16[4,1,144,384]{3,2,1,0:T(8,128)(2,1)S(1)} collective-permute-done((bf16[4,1,144,384]{3,2,1,0:T(8,128)(2,1)S(1)}, bf16[4,1,144,384]{3,2,1,0:T(8,128)(2,1)S(1)}, u32[]{:S(2)}, u32[]{:S(2)}) %collective-permute-start.16) | collective-permute-done | bytes 442400 | tf_op jit(solution)/shard_map/ppermute | solution.py:475
  373.4 4.1 collective-permute-done.17
  377.6 2.3 collective-permute-start.18
  381.9 2.6 collective-permute-done.18
  387.2 2.2 fusion.11
  391.0 15.5 %multiply_reduce_fusion.1 = (f32[]{:T(128)}, f32[1024,1000]{0,1:T(8,128)}) fusion(f32[1024,1000]{0,1:T(8,128)S(1)} %copy-done.1, f32[]{:T(128)S(6)} %div.51, bf16[768,1384]{1,0:T(8,128)(2,1)} %all-gather.12.cloned.1.call-done, f32[768,1024]{1,0:T(8,128)S(1)} %fusion.11), kind=kOutput, calls=%fused_computation.7 | convolution fusion | flops 1578770432 | bytes 12910600 | tf_op jit(solution)/shard_map/dot_general | solution.py:30
  406.5 17.6 %multiply_reduce_fusion.2 = (f32[]{:T(128)}, f32[384,1024]{1,0:T(8,128)}) fusion(f32[]{:T(128)S(6)} %div.51, f32[768,1024]{1,0:T(8,128)} %copy-done.7, bf16[768,1384]{1,0:T(8,128)(2,1)} %all-gather.12.cloned.1.call-done, f32[1024,1000]{0,1:T(8,128)} %param.58), kind=kOutput, calls=%fused_computation.27 | convolution fusion | flops 2181406720 | bytes 10940424 | tf_op jit(solution)/shard_map/dot_general | solution.py:30
  431.9 4.0 all-to-all-start.2
  436.8 7.3 %all-to-all-done.2 = f32[32,8,128]{2,1,0:T(8,128)S(1)} async-done(((f32[32,8,128]{2,1,0:T(8,128)}), f32[32,8,128]{2,1,0:T(8,128)S(1)}, u32[]{:S(2)}, u32[]{:S(2)}) %all-to-all-start.2) | async-done | bytes 131104 | tf_op jit(solution)/shard_map/all_to_all | solution.py:517
  445.5 2.5 fusion.42
  448.9 1.9 copy.186
  450.8 1.9 copy.187
  458.2 5.5 %fusion.36 = (bf16[384,1024]{1,0:T(8,128)(2,1)}, f32[384,1024]{1,0:T(8,128)S(1)}, f32[384,1024]{1,0:T(8,128)}, f32[384,1024]{1,0:T(8,128)}) fusion(f32[384,1024]{1,0:T(8,128)S(1)} %copy-done.4, f32[384,1024]{1,0:T(8,128)} %get-tuple-element.374, f32[]{:T(128)S(6)} %min.3, f32[384,1024]{1,0:T(8,128)} %param.55, f32[384,1024]{1,0:T(8,128)} %param.56), kind=kLoop, calls=%fused_computation.155 | loop fusion | flops 6291456 | bytes 11796484 | tf_op jit(solution)/shard_map/convert_element_type | solution.py:529
  467.3 7.6 %fusion.34 = (bf16[1024,1000]{0,1:T(8,128)(2,1)}, f32[1024,1000]{0,1:T(8,128)S(1)}, f32[1024,1000]{0,1:T(8,128)}, f32[1024,1000]{0,1:T(8,128)}) fusion(f32[1024,1000]{0,1:T(8,128)S(1)} %copy-done.2, f32[1024,1000]{0,1:T(8,128)S(1)} %copy-done.5, f32[]{:T(128)S(6)} %min.3, f32[1024,1000]{0,1:T(8,128)S(1)} %copy-done.11, f32[1024,1000]{0,1:T(8,128)} %param.60), kind=kLoop, calls=%fused_computation.154 | loop fusion | flops 16384000 | bytes 30720004 | tf_op jit(solution)/shard_map/convert_element_type | solution.py:529
  474.9 2.0 copy-done.6
  476.9 2.9 add_multiply_fusion
  483.3 6.4 %fusion.38 = (bf16[3,384,576]{1,2,0:T(8,128)(2,1)}, f32[3,384,576]{1,2,0:T(8,128)S(1)}, f32[3,384,576]{1,2,0:T(8,128)}, f32[3,384,576]{1,2,0:T(8,128)}) fusion(f32[3,384,576]{1,2,0:T(8,128)S(1)} %copy-done.15, f32[3,3,4,48,384]{4,3,2,1,0:T(8,128)S(1)} %multiply_multiply_fusion.2, f32[3,384,576]{1,2,0:T(8,128)S(1)} %copy-done.17, f32[3,384,576]{1,2,0:T(8,128)} %param.52), kind=kLoop, calls=%fused_computation.156 | loop fusion | flops 9953280 | bytes 19906560 | tf_op jit(solution)/shard_map/convert_element_type | solution.py:529
  489.7 1.9 add_multiply_fusion.1
  (258 shorter events, 94.0 us)
Async XLA Ops:
  7.2 96.3 %all-gather.10.cloned.1.call-start = ((), (), s32[]{:S(2)}) async-start(), calls=%async_computation.3 | async-start | bytes 10948608 | tf_op jit(solution)/shard_map/all_gather | solution.py:588
  11.8 81.6 %all-to-all-start.1 = ((f32[32,8,128]{2,1,0:T(8,128)}), f32[32,8,128]{2,1,0:T(8,128)S(1)}, u32[]{:S(2)}, u32[]{:S(2)}) async-start(f32[32,8,128]{2,1,0:T(8,128)} %broadcast_in_dim.53), calls=%async_computation.1 | async-start | bytes 262144 | tf_op jit(solution)/shard_map/all_to_all | solution.py:517
  22.2 46.3 %copy-start.36 = (s32[4]{0:T(128)S(1)}, s32[4]{0:T(128)}, u32[]{:S(2)}) copy-start(s32[4]{0:T(128)} %param.41) | copy-start | bytes 52
  22.2 46.9 %copy-start.39 = (pred[24]{0:T(512)(128)(4,1)S(1)}, pred[24]{0:T(512)(128)(4,1)}, u32[]{:S(2)}) copy-start(pred[24]{0:T(512)(128)(4,1)} %constant.302) | copy-start | bytes 76
  22.2 46.9 %copy-start.40 = (pred[24]{0:T(512)(128)(4,1)S(1)}, pred[24]{0:T(512)(128)(4,1)}, u32[]{:S(2)}) copy-start(pred[24]{0:T(512)(128)(4,1)} %constant.303) | copy-start | bytes 76
  22.2 46.9 %copy-start.41 = (pred[24]{0:T(512)(128)(4,1)S(1)}, pred[24]{0:T(512)(128)(4,1)}, u32[]{:S(2)}) copy-start(pred[24]{0:T(512)(128)(4,1)} %constant.304) | copy-start | bytes 76
  22.2 49.5 %copy-start.38 = (s32[24]{0:T(128)S(1)}, s32[24]{0:T(128)}, u32[]{:S(2)}) copy-start(s32[24]{0:T(128)} %param.40) | copy-start | bytes 292
  22.2 54.7 %copy-start.42 = (s32[24]{0:T(128)S(1)}, s32[24]{0:T(128)}, u32[]{:S(2)}) copy-start(s32[24]{0:T(128)} %param.39) | copy-start | bytes 292
  22.2 56.6 %copy-start.43 = (s32[2]{0:T(128)S(1)}, s32[2]{0:T(128)}, u32[]{:S(2)}) copy-start(s32[2]{0:T(128)} %constant.274.clone.1) | copy-start | bytes 28
  68.3 15.2 %copy-start.12 = (bf16[48,8,4,256]{3,1,2,0:T(8,128)(2,1)}, bf16[48,8,4,256]{3,1,2,0:T(8,128)(2,1)S(1)}, u32[]{:S(2)}) copy-start(bf16[48,8,4,256]{3,1,2,0:T(8,128)(2,1)S(1)} %copy.192) | copy-start | bytes 2359300
  138.7 14.8 %copy-start.4 = (f32[384,1024]{1,0:T(8,128)S(1)}, f32[384,1024]{1,0:T(8,128)}, u32[]{:S(2)}) copy-start(f32[384,1024]{1,0:T(8,128)} %param.54) | copy-start | bytes 4718596
  138.7 15.1 %copy-start = (f32[1024,1000]{0,1:T(8,128)S(1)}, f32[1024,1000]{0,1:T(8,128)}, u32[]{:S(2)}) copy-start(f32[1024,1000]{0,1:T(8,128)} %param.58) | copy-start | bytes 12288004
  169.8 8.1 %all-to-all-start = ((f32[4,24,384]{2,1,0:T(8,128)}), f32[4,24,384]{2,1,0:T(8,128)S(1)}, u32[]{:S(2)}, u32[]{:S(2)}) async-start(f32[4,24,384]{2,1,0:T(8,128)} %bitcast.21), calls=%async_computation | async-start | bytes 294912 | tf_op jit(solution)/shard_map/all_to_all | solution.py:617
  173.2 214.0 %all-gather.12.cloned.1.call-start = ((), (), s32[]{:S(2)}) async-start(), calls=%async_computation.4 | async-start | bytes 2230272 | tf_op jit(solution)/shard_map/all_gather | solution.py:621
  243.2 21.6 %copy-start.32 = (f32[8,384]{1,0:T(8,128)S(1)}, f32[8,384]{1,0:T(8,128)}, u32[]{:S(2)}) copy-start(f32[8,384]{1,0:T(8,128)} %get-tuple-element.151) | copy-start | bytes 36868
  268.4 3.5 collective-permute-start.19
  269.7 35.5 %collective-permute-start.2 = (bf16[16,96,384]{2,1,0:T(8,128)(2,1)}, bf16[16,96,384]{2,1,0:T(8,128)(2,1)}, u32[]{:S(2)}, u32[]{:S(2)}) collective-permute-start(bf16[16,96,384]{2,1,0:T(8,128)(2,1)} %constant_dynamic-slice_fusion.22), channel_id=1, source_target_pairs={{0,1},{1,0},{2,3},{3,2},{4,5},{5,4},{6,7},{7,6},{8,9},{9,8},{10,11... | collective-permute-start | bytes 3538952 | tf_op jit(solution)/shard_map/ppermute | solution.py:475
  270.2 9.1 %collective-permute-start = (bf16[8,96,384]{2,1,0:T(8,128)(2,1)S(1)}, bf16[8,96,384]{2,1,0:T(8,128)(2,1)}, u32[]{:S(2)}, u32[]{:S(2)}) collective-permute-start(bf16[8,96,384]{2,1,0:T(8,128)(2,1)S(1)} %constant_dynamic-slice_fusion.24), channel_id=1, source_target_pairs={{0,1},{1,0},{2,3},{3,2},{4,5},{5,4},{6,7},{7,6},{8,9},{9,8},{10,11... | collective-permute-start | bytes 1769480 | tf_op jit(solution)/shard_map/ppermute | solution.py:475
  271.6 37.5 %collective-permute-start.9 = (bf16[16,96,384]{2,1,0:T(8,128)(2,1)}, bf16[16,96,384]{2,1,0:T(8,128)(2,1)}, u32[]{:S(2)}, u32[]{:S(2)}) collective-permute-start(bf16[16,96,384]{2,1,0:T(8,128)(2,1)} %constant_dynamic-slice_fusion.15), channel_id=1, source_target_pairs={{0,1},{1,0},{2,3},{3,2},{4,5},{5,4},{6,7},{7,6},{8,9},{9,8},{10,11... | collective-permute-start | bytes 3538952 | tf_op jit(solution)/shard_map/ppermute | solution.py:475
  272.1 7.0 %collective-permute-start.20 = (bf16[384,256]{0,1:T(8,128)(2,1)S(1)}, bf16[384,256]{0,1:T(8,128)(2,1)S(1)}, u32[]{:S(2)}, u32[]{:S(2)}) collective-permute-start(bf16[384,256]{0,1:T(8,128)(2,1)S(1)} %constant_dynamic-slice_fusion.4), channel_id=1, source_target_pairs={{0,2},{1,3},{2,0},{3,1},{4,6},{5,7},{6,4},{7,5},{8,10},{9,11},{10,... | collective-permute-start | bytes 589832 | tf_op jit(solution)/shard_map/ppermute | solution.py:475
  273.4 11.7 %collective-permute-start.7 = (bf16[8,96,384]{2,1,0:T(8,128)(2,1)}, bf16[8,96,384]{2,1,0:T(8,128)(2,1)}, u32[]{:S(2)}, u32[]{:S(2)}) collective-permute-start(bf16[8,96,384]{2,1,0:T(8,128)(2,1)} %constant_dynamic-slice_fusion.17), channel_id=1, source_target_pairs={{0,1},{1,0},{2,3},{3,2},{4,5},{5,4},{6,7},{7,6},{8,9},{9,8},{10,11... | collective-permute-start | bytes 1769480 | tf_op jit(solution)/shard_map/ppermute | solution.py:475
  279.1 58.5 %collective-permute-start.14 = (bf16[24,96,384]{2,1,0:T(8,128)(2,1)}, bf16[24,96,384]{2,1,0:T(8,128)(2,1)}, u32[]{:S(2)}, u32[]{:S(2)}) collective-permute-start(bf16[24,96,384]{2,1,0:T(8,128)(2,1)} %constant_dynamic-slice_fusion.10), channel_id=1, source_target_pairs={{0,1},{1,0},{2,3},{3,2},{4,5},{5,4},{6,7},{7,6},{8,9},{9,8},{10,11... | collective-permute-start | bytes 5308424 | tf_op jit(solution)/shard_map/ppermute | solution.py:475
  279.4 5.3 %collective-permute-start.21 = (bf16[4,1,48,256]{3,2,1,0:T(8,128)(2,1)S(1)}, bf16[4,1,48,256]{3,2,1,0:T(8,128)(2,1)S(1)}, u32[]{:S(2)}, u32[]{:S(2)}) collective-permute-start(bf16[4,1,48,256]{3,2,1,0:T(8,128)(2,1)S(1)} %constant_dynamic-slice_fusion.3), channel_id=1, source_target_pairs={{0,4},{4,0},{8,12},{12,8},{16,20},{20,16},{24,28},{28,24},{1,5},{5... | collective-permute-start | bytes 294920 | tf_op jit(solution)/shard_map/ppermute | solution.py:475
  284.7 19.4 %collective-permute-start.1 = (bf16[8,48,384]{2,1,0:T(8,128)(2,1)}, bf16[8,48,384]{2,1,0:T(8,128)(2,1)}, u32[]{:S(2)}, u32[]{:S(2)}) collective-permute-start(bf16[8,48,384]{2,1,0:T(8,128)(2,1)} %constant_dynamic-slice_fusion.23), channel_id=1, source_target_pairs={{0,2},{1,3},{2,0},{3,1},{4,6},{5,7},{6,4},{7,5},{8,10},{9,11},{10,... | collective-permute-start | bytes 884744 | tf_op jit(solution)/shard_map/ppermute | solution.py:475
  285.1 4.2 collective-permute-start.22
  289.3 4.8 collective-permute-start.23
  294.0 17.1 %collective-permute-start.8 = (bf16[8,48,384]{2,1,0:T(8,128)(2,1)}, bf16[8,48,384]{2,1,0:T(8,128)(2,1)}, u32[]{:S(2)}, u32[]{:S(2)}) collective-permute-start(bf16[8,48,384]{2,1,0:T(8,128)(2,1)} %constant_dynamic-slice_fusion.16), channel_id=1, source_target_pairs={{0,2},{1,3},{2,0},{3,1},{4,6},{5,7},{6,4},{7,5},{8,10},{9,11},{10,... | collective-permute-start | bytes 884744 | tf_op jit(solution)/shard_map/ppermute | solution.py:475
  307.3 16.2 %collective-permute-start.3 = (bf16[16,48,384]{2,1,0:T(8,128)(2,1)S(1)}, bf16[16,48,384]{2,1,0:T(8,128)(2,1)S(1)}, u32[]{:S(2)}, u32[]{:S(2)}) collective-permute-start(bf16[16,48,384]{2,1,0:T(8,128)(2,1)S(1)} %constant_dynamic-slice_fusion.21), channel_id=1, source_target_pairs={{0,2},{1,3},{2,0},{3,1},{4,6},{5,7},{6,4},{7,5},{8,10},{9,11},{10,... | collective-permute-start | bytes 1769480 | tf_op jit(solution)/shard_map/ppermute | solution.py:475
  310.8 24.9 %collective-permute-start.10 = (bf16[16,48,384]{2,1,0:T(8,128)(2,1)S(1)}, bf16[16,48,384]{2,1,0:T(8,128)(2,1)S(1)}, u32[]{:S(2)}, u32[]{:S(2)}) collective-permute-start(bf16[16,48,384]{2,1,0:T(8,128)(2,1)S(1)} %constant_dynamic-slice_fusion.14), channel_id=1, source_target_pairs={{0,2},{1,3},{2,0},{3,1},{4,6},{5,7},{6,4},{7,5},{8,10},{9,11},{10,... | collective-permute-start | bytes 1769480 | tf_op jit(solution)/shard_map/ppermute | solution.py:475
  323.9 13.7 %copy-start.14 = (bf16[4608,384]{1,0:T(8,128)(2,1)S(1)}, bf16[4608,384]{1,0:T(8,128)(2,1)}, u32[]{:S(2)}) copy-start(bf16[4608,384]{1,0:T(8,128)(2,1)} %get-tuple-element.144) | copy-start | bytes 10616836
  323.9 17.4 %collective-permute-start.4 = (bf16[4,1,144,384]{3,2,1,0:T(8,128)(2,1)S(1)}, bf16[4,1,144,384]{3,2,1,0:T(8,128)(2,1)S(1)}, u32[]{:S(2)}, u32[]{:S(2)}) collective-permute-start(bf16[4,1,144,384]{3,2,1,0:T(8,128)(2,1)S(1)} %constant_dynamic-slice_fusion.20), channel_id=1, source_target_pairs={{0,4},{4,0},{8,12},{12,8},{16,20},{20,16},{24,28},{28,24},{1,5},{5... | collective-permute-start | bytes 1327112 | tf_op jit(solution)/shard_map/ppermute | solution.py:475
  336.0 11.7 %collective-permute-start.11 = (bf16[4,1,144,384]{3,2,1,0:T(8,128)(2,1)S(1)}, bf16[4,1,144,384]{3,2,1,0:T(8,128)(2,1)S(1)}, u32[]{:S(2)}, u32[]{:S(2)}) collective-permute-start(bf16[4,1,144,384]{3,2,1,0:T(8,128)(2,1)S(1)} %constant_dynamic-slice_fusion.13), channel_id=1, source_target_pairs={{0,4},{4,0},{8,12},{12,8},{16,20},{20,16},{24,28},{28,24},{1,5},{5... | collective-permute-start | bytes 1327112 | tf_op jit(solution)/shard_map/ppermute | solution.py:475
  339.7 20.9 %collective-permute-start.15 = (bf16[24,48,384]{2,1,0:T(8,128)(2,1)S(1)}, bf16[24,48,384]{2,1,0:T(8,128)(2,1)S(1)}, u32[]{:S(2)}, u32[]{:S(2)}) collective-permute-start(bf16[24,48,384]{2,1,0:T(8,128)(2,1)S(1)} %constant_dynamic-slice_fusion.9), channel_id=1, source_target_pairs={{0,2},{1,3},{2,0},{3,1},{4,6},{5,7},{6,4},{7,5},{8,10},{9,11},{10,... | collective-permute-start | bytes 2654216 | tf_op jit(solution)/shard_map/ppermute | solution.py:475
  341.5 7.7 %collective-permute-start.5 = (bf16[2,1,144,384]{3,2,1,0:T(8,128)(2,1)S(1)}, bf16[2,1,144,384]{3,2,1,0:T(8,128)(2,1)S(1)}, u32[]{:S(2)}, u32[]{:S(2)}) collective-permute-start(bf16[2,1,144,384]{3,2,1,0:T(8,128)(2,1)S(1)} %constant_dynamic-slice_fusion.19), channel_id=1, source_target_pairs={{0,8},{4,12},{8,0},{12,4},{16,24},{20,28},{24,16},{28,20},{1,9},{5... | collective-permute-start | bytes 663560 | tf_op jit(solution)/shard_map/ppermute | solution.py:475
  347.8 15.5 %collective-permute-start.12 = (bf16[2,1,144,384]{3,2,1,0:T(8,128)(2,1)S(1)}, bf16[2,1,144,384]{3,2,1,0:T(8,128)(2,1)S(1)}, u32[]{:S(2)}, u32[]{:S(2)}) collective-permute-start(bf16[2,1,144,384]{3,2,1,0:T(8,128)(2,1)S(1)} %constant_dynamic-slice_fusion.12), channel_id=1, source_target_pairs={{0,8},{4,12},{8,0},{12,4},{16,24},{20,28},{24,16},{28,20},{1,9},{5... | collective-permute-start | bytes 663560 | tf_op jit(solution)/shard_map/ppermute | solution.py:475
  360.9 10.5 %collective-permute-start.16 = (bf16[4,1,144,384]{3,2,1,0:T(8,128)(2,1)S(1)}, bf16[4,1,144,384]{3,2,1,0:T(8,128)(2,1)S(1)}, u32[]{:S(2)}, u32[]{:S(2)}) collective-permute-start(bf16[4,1,144,384]{3,2,1,0:T(8,128)(2,1)S(1)} %constant_dynamic-slice_fusion.8), channel_id=1, source_target_pairs={{0,4},{4,0},{8,12},{12,8},{16,20},{20,16},{24,28},{28,24},{1,5},{5... | collective-permute-start | bytes 1327112 | tf_op jit(solution)/shard_map/ppermute | solution.py:475
  361.4 11.3 %collective-permute-start.6 = (bf16[1,1,144,384]{3,2,1,0:T(8,128)(2,1)S(1)}, bf16[1,1,144,384]{3,2,1,0:T(8,128)(2,1)S(1)}, u32[]{:S(2)}, u32[]{:S(2)}) collective-permute-start(bf16[1,1,144,384]{3,2,1,0:T(8,128)(2,1)S(1)} %constant_dynamic-slice_fusion.18), channel_id=1, source_target_pairs={{0,16},{4,20},{8,24},{12,28},{16,0},{20,4},{24,8},{28,12},{1,17},{... | collective-permute-start | bytes 331784 | tf_op jit(solution)/shard_map/ppermute | solution.py:475
  363.4 16.6 %collective-permute-start.13 = (bf16[1,1,144,384]{3,2,1,0:T(8,128)(2,1)S(1)}, bf16[1,1,144,384]{3,2,1,0:T(8,128)(2,1)S(1)}, u32[]{:S(2)}, u32[]{:S(2)}) collective-permute-start(bf16[1,1,144,384]{3,2,1,0:T(8,128)(2,1)S(1)} %constant_dynamic-slice_fusion.11), channel_id=1, source_target_pairs={{0,16},{4,20},{8,24},{12,28},{16,0},{20,4},{24,8},{28,12},{1,17},{... | collective-permute-start | bytes 331784 | tf_op jit(solution)/shard_map/ppermute | solution.py:475
  371.5 6.0 %collective-permute-start.17 = (bf16[2,1,144,384]{3,2,1,0:T(8,128)(2,1)S(1)}, bf16[2,1,144,384]{3,2,1,0:T(8,128)(2,1)S(1)}, u32[]{:S(2)}, u32[]{:S(2)}) collective-permute-start(bf16[2,1,144,384]{3,2,1,0:T(8,128)(2,1)S(1)} %constant_dynamic-slice_fusion.7), channel_id=1, source_target_pairs={{0,8},{4,12},{8,0},{12,4},{16,24},{20,28},{24,16},{28,20},{1,9},{5... | collective-permute-start | bytes 663560 | tf_op jit(solution)/shard_map/ppermute | solution.py:475
  377.6 6.9 %collective-permute-start.18 = (bf16[1,1,144,384]{3,2,1,0:T(8,128)(2,1)S(1)}, bf16[1,1,144,384]{3,2,1,0:T(8,128)(2,1)S(1)}, u32[]{:S(2)}, u32[]{:S(2)}) collective-permute-start(bf16[1,1,144,384]{3,2,1,0:T(8,128)(2,1)S(1)} %constant_dynamic-slice_fusion.6), channel_id=1, source_target_pairs={{0,16},{4,20},{8,24},{12,28},{16,0},{20,4},{24,8},{28,12},{1,17},{... | collective-permute-start | bytes 331784 | tf_op jit(solution)/shard_map/ppermute | solution.py:475
  406.5 29.5 %copy-start.26 = (bf16[1,1,144,384]{3,2,1,0:T(8,128)(2,1)S(1)}, bf16[1,1,144,384]{3,2,1,0:T(8,128)(2,1)}, u32[]{:S(2)}) copy-start(bf16[1,1,144,384]{3,2,1,0:T(8,128)(2,1)} %get-tuple-element.343) | copy-start | bytes 331780
  431.9 12.2 %all-to-all-start.2 = ((f32[32,8,128]{2,1,0:T(8,128)}), f32[32,8,128]{2,1,0:T(8,128)S(1)}, u32[]{:S(2)}, u32[]{:S(2)}) async-start(f32[32,8,128]{2,1,0:T(8,128)} %broadcast_in_dim.55), calls=%async_computation.2 | async-start | bytes 262144 | tf_op jit(solution)/shard_map/all_to_all | solution.py:517
  435.9 43.9 %all-gather.14.cloned.1.call-start = ((), (), s32[]{:S(2)}) async-start(), calls=%async_computation.5 | async-start | bytes 1658880 | tf_op jit(solution)/shard_map/all_gather | solution.py:505
  448.9 8.6 %copy-start.31 = (f32[14,48]{1,0:T(8,128)S(1)}, f32[14,48]{1,0:T(8,128)}, u32[]{:S(2)}) copy-start(f32[14,48]{1,0:T(8,128)} %param.46) | copy-start | bytes 8068
  448.9 8.7 %copy-start.33 = (f32[14,48]{1,0:T(8,128)S(1)}, f32[14,48]{1,0:T(8,128)}, u32[]{:S(2)}) copy-start(f32[14,48]{1,0:T(8,128)} %param.47) | copy-start | bytes 8068
  448.9 8.7 %copy-start.34 = (f32[14,48]{1,0:T(8,128)S(1)}, f32[14,48]{1,0:T(8,128)}, u32[]{:S(2)}) copy-start(f32[14,48]{1,0:T(8,128)} %param.48) | copy-start | bytes 8068
  458.2 7.8 %copy-start.11 = (f32[1024,1000]{0,1:T(8,128)S(1)}, f32[1024,1000]{0,1:T(8,128)}, u32[]{:S(2)}) copy-start(f32[1024,1000]{0,1:T(8,128)} %param.59) | copy-start | bytes 12288004
  467.3 9.6 %copy-start.10 = (f32[1024,1000]{0,1:T(8,128)S(1)}, f32[1024,1000]{0,1:T(8,128)}, u32[]{:S(2)}) copy-start(f32[1024,1000]{0,1:T(8,128)} %param.61) | copy-start | bytes 12288004
  (26 other events, 109.5 us)
Sparse Core Ops, SparseCore 0:
  11.5 91.9 all-gather.9
  177.4 56.6 all-gather.11
  438.8 19.5 all-gather.13

commit v2 on v1

--- a/solution.py
+++ b/solution.py
@@ -1,3 +1,4 @@
+import functools
 import math
 import jax
 import jax.numpy as jnp
@@ -132,6 +133,10 @@
     return pltpu.CompilerParams(dimension_semantics=("arbitrary",) * n, vmem_limit_bytes=mb << 20)
 
 
+def lasting(us):
+    return pl.CostEstimate(flops=int(us * 1e9), bytes_accessed=int(us * 2e6), transcendentals=0)
+
+
 def layer_forward(x, w, layer, gains, seg, step_rows=512):
     rows = x.shape[0]
     steps = rows // step_rows
@@ -153,6 +158,7 @@
             jax.ShapeDtypeStruct((rows, D), f32),
         ],
         compiler_params=params(),
+        cost_estimate=lasting(17),
         name="layer_fwd",
     )(x, w, w, w, gains, seg[:, None], seg.reshape(steps, 1, step_rows))
 
@@ -183,6 +189,7 @@
             jax.ShapeDtypeStruct((rows, D), f32),
         ],
         compiler_params=params(),
+        cost_estimate=lasting(18),
         name="first_fwd",
     )(patches, pos[:, None], e, w, w, w, gains, seg[:, None], seg.reshape(steps, 1, step_rows))
 
@@ -221,6 +228,16 @@
     feat_ref[...] = (u3 * g3 + b3).astype(bf16)
 
 
+def put_halves(core_ref, acc_ref, keep_ref, send_ref):
+    half = keep_ref.shape[1]
+    mine = core_ref[0] * half
+    other = (1 - core_ref[0]) * half
+    for i in range(keep_ref.shape[0]):
+        base = i * 2 * half
+        keep_ref[i] = acc_ref[pl.ds(base + mine, half), :].astype(bf16)
+        send_ref[i] = acc_ref[pl.ds(base + other, half), :].astype(bf16)
+
+
 def smem_spec():
     return pl.BlockSpec(memory_space=pltpu.SMEM)
 
@@ -246,11 +263,12 @@
             jax.ShapeDtypeStruct((slots, D), bf16),
         ],
         compiler_params=params(),
+        cost_estimate=lasting(9),
         name="last_fwd",
     )(cls, x, w, w, w, gains, seg[None, :], seg_cls[:, None])
 
 
-def last_bwd_kernel(cls_ref, df_ref, x_ref, wa_ref, wu_ref, wd_ref, g_ref, sk_ref, sq_ref, kv_ref, xc_ref, q_ref, att_ref, x1_ref, xo_ref, dx_ref, dw_ref, dv_ref, dn_ref):
+def last_bwd_kernel(cls_ref, core_ref, df_ref, x_ref, wa_ref, wu_ref, wd_ref, g_ref, sk_ref, sq_ref, kv_ref, xc_ref, q_ref, att_ref, x1_ref, xo_ref, dx_ref, keep_ref, send_ref, dv_ref, dn_ref, dw_ref):
     g1, b1, g2, b2, g3, b3 = (g_ref[i : i + 1, :] for i in range(6))
     slots = xc_ref.shape[0]
     df = df_ref[...]
@@ -263,15 +281,15 @@
     second = (u2 * g2 + b2).astype(bf16)
     value, slope = gelu_both(nt(second, wu_ref[...]))
     dpre = (nt(branch, wd_ref[...]) * slope).astype(bf16)
-    dw_ref[4 * D + MLP :, :] = tn(value.astype(bf16), branch).astype(bf16)
-    dw_ref[4 * D : 4 * D + MLP, :] = tn(dpre, second).astype(bf16)
+    dw_ref[4 * D + MLP :, :] = tn(value.astype(bf16), branch)
+    dw_ref[4 * D : 4 * D + MLP, :] = tn(dpre, second)
     dsecond = nn(dpre, wu_ref[...])
     dg2 = jnp.sum(dsecond * u2, axis=0, keepdims=True)
     db2 = jnp.sum(dsecond, axis=0, keepdims=True)
     dx1 = dxo + unit_back(u2, i2, g2, dsecond)
     ab = dx1.astype(bf16)
     datt = nn(ab, wa_ref[3 * D :, :]).astype(bf16)
-    dw_ref[3 * D : 4 * D, :] = tn(ab, att_ref[...]).astype(bf16)
+    dw_ref[3 * D : 4 * D, :] = tn(ab, att_ref[...])
     same = sq_ref[...] == sk_ref[...]
     q, kv = q_ref[...], kv_ref[...]
     dqs, dks, dvs = [], [], []
@@ -290,9 +308,9 @@
     dkv = jnp.concatenate(dks + dvs, axis=1).astype(bf16)
     u, i1 = unit(x_ref[...])
     normed = (u * g1 + b1).astype(bf16)
-    dw_ref[D : 3 * D, :] = tn(dkv, normed).astype(bf16)
+    dw_ref[D : 3 * D, :] = tn(dkv, normed)
     uc, _ = unit(xc_ref[...])
-    dw_ref[:D, :] = tn(dq, (uc * g1 + b1).astype(bf16)).astype(bf16)
+    dw_ref[:D, :] = tn(dq, (uc * g1 + b1).astype(bf16))
     dn_ref[...] = nn(dkv, wa_ref[D : 3 * D, :])
     dnc = nn(dq, wa_ref[:D, :])
     for i in range(slots):
@@ -306,27 +324,29 @@
         at = pl.ds(cls_ref[i], 1)
         dx_ref[at, :] = dx_ref[at, :] + dx1[i : i + 1, :]
     dv_ref[...] = jnp.concatenate([dg1, db1, dg2, db2, dg3, db3, jnp.zeros((2, D), f32)], axis=0)
-
-
-def last_backward(cls, df, x, w, layer, gains, seg, seg_cls, kv, xc, q, att, x1, xo):
+    put_halves(core_ref, dw_ref, keep_ref, send_ref)
+
+
+def last_backward(cls, core, wide, df, x, w, layer, gains, seg, seg_cls, kv, xc, q, att, x1, xo):
     rows = x.shape[0]
     return pl.pallas_call(
         last_bwd_kernel,
         grid=(1,),
-        in_specs=[smem_spec(), vmem_spec(), whole_spec(x.shape), *(third_spec(3 * layer + i) for i in range(3)), *[vmem_spec()] * 9],
-        out_specs=[vmem_spec()] * 3,
+        in_specs=[smem_spec(), smem_spec(), vmem_spec(), whole_spec(x.shape), *(third_spec(3 * layer + i) for i in range(3)), *[vmem_spec()] * 9],
+        out_specs=[vmem_spec()] * 4,
         out_shape=[
             jax.ShapeDtypeStruct((rows, D), f32),
-            jax.ShapeDtypeStruct((12 * D, D), bf16),
+            *[jax.ShapeDtypeStruct((12 * D // wide, wide // 2, D), bf16)] * 2,
             jax.ShapeDtypeStruct((8, D), f32),
         ],
-        scratch_shapes=[pltpu.VMEM((rows, D), f32)],
+        scratch_shapes=[pltpu.VMEM((rows, D), f32), pltpu.VMEM((12 * D, D), f32)],
         compiler_params=params(),
+        cost_estimate=lasting(15),
         name="last_bwd",
-    )(cls, df, x, w, w, w, gains, seg[None, :], seg_cls[:, None], kv, xc, q, att, x1, xo)
-
-
-def mlp_bwd_kernel(dxo_ref, x1_ref, wu_ref, wd_ref, g_ref, dx1_ref, dw_ref, dv_ref, acc_ref):
+    )(cls, core, df, x, w, w, w, gains, seg[None, :], seg_cls[:, None], kv, xc, q, att, x1, xo)
+
+
+def mlp_bwd_kernel(core_ref, dxo_ref, x1_ref, att_ref, wu_ref, wd_ref, g_ref, dx1_ref, keep_ref, send_ref, dv_ref, acc_ref):
     step = pl.program_id(0)
     g2, b2 = g_ref[2:3, :], g_ref[3:4, :]
     dxo = dxo_ref[...]
@@ -338,42 +358,52 @@
     dpre = (nt(branch, wd_ref[...]) * slope).astype(bf16)
     dsecond = nn(dpre, wu_ref[...])
     sums = jnp.concatenate([jnp.sum(dsecond * u2, axis=0, keepdims=True), jnp.sum(dsecond, axis=0, keepdims=True), jnp.zeros((6, D), f32)], axis=0)
-    dx1_ref[...] = dxo + unit_back(u2, i2, g2, dsecond)
+    dx1 = dxo + unit_back(u2, i2, g2, dsecond)
+    dx1_ref[...] = dx1
+    ab = dx1.astype(bf16)
     last = pl.num_programs(0) - 1
 
     @pl.when(step == 0)
     def _():
-        acc_ref[:MLP, :] = tn(dpre, second)
-        acc_ref[MLP:, :] = tn(hidden, branch)
+        acc_ref[:D, :] = tn(ab, att_ref[...])
+        acc_ref[D : D + MLP, :] = tn(dpre, second)
+        acc_ref[D + MLP :, :] = tn(hidden, branch)
         dv_ref[...] = sums
 
     @pl.when(step > 0)
     def _():
-        acc_ref[:MLP, :] += tn(dpre, second)
-        acc_ref[MLP:, :] += tn(hidden, branch)
+        acc_ref[:D, :] += tn(ab, att_ref[...])
+        acc_ref[D : D + MLP, :] += tn(dpre, second)
+        acc_ref[D + MLP :, :] += tn(hidden, branch)
         dv_ref[...] += sums
 
     @pl.when(step == last)
     def _():
-        dw_ref[...] = acc_ref[...].astype(bf16)
-
-
-def mlp_backward(dxo, x1, w, layer, gains, step_rows=512):
+        put_halves(core_ref, acc_ref, keep_ref, send_ref)
+
+
+def mlp_backward(core, wide, dxo, x1, att, w, layer, gains, step_rows=512):
     rows = x1.shape[0]
     steps = rows // step_rows
     return pl.pallas_call(
         mlp_bwd_kernel,
         grid=(steps,),
-        in_specs=[rows_spec(step_rows, D), rows_spec(step_rows, D), third_spec(3 * layer + 1), third_spec(3 * layer + 2), whole_spec(gains.shape)],
-        out_specs=[rows_spec(step_rows, D), whole_spec((2 * MLP, D)), whole_spec((8, D))],
-        out_shape=[jax.ShapeDtypeStruct((rows, D), f32), jax.ShapeDtypeStruct((2 * MLP, D), bf16), jax.ShapeDtypeStruct((8, D), f32)],
-        scratch_shapes=[pltpu.VMEM((2 * MLP, D), f32)],
+        in_specs=[smem_spec(), *[rows_spec(step_rows, D)] * 3, third_spec(3 * layer + 1), third_spec(3 * layer + 2), whole_spec(gains.shape)],
+        out_specs=[rows_spec(step_rows, D), *[whole_spec((9 * D // wide, wide // 2, D))] * 2, whole_spec((8, D))],
+        out_shape=[jax.ShapeDtypeStruct((rows, D), f32), *[jax.ShapeDtypeStruct((9 * D // wide, wide // 2, D), bf16)] * 2, jax.ShapeDtypeStruct((8, D), f32)],
+        scratch_shapes=[pltpu.VMEM((9 * D, D), f32)],
         compiler_params=params(),
+        cost_estimate=lasting(16),
         name="mlp_bwd",
-    )(dxo, x1, w, w, gains)
-
-
-def att_bwd_kernel(dx1_ref, x_ref, qkv_ref, att_ref, w_ref, g_ref, sc_ref, sr_ref, dx_ref, dw_ref, dv_ref, acc_ref):
+    )(core, dxo, x1, att, w, w, gains)
+
+
+def att_bwd_kernel(first_vec, *refs):
+    core_ref, dx1_ref, x_ref, qkv_ref, w_ref, g_ref, sc_ref, sr_ref, *refs = refs
+    if first_vec:
+        in_ref, vec_ref, keep_ref, send_ref, tkeep_ref, tsend_ref, acc_ref, dv_ref, table_ref = refs
+    else:
+        dx_ref, keep_ref, send_ref, dv_ref, acc_ref = refs
     step = pl.program_id(0)
     g1, b1 = g_ref[0:1, :], g_ref[1:2, :]
     dx1 = dx1_ref[...]
@@ -404,48 +434,183 @@
     normed = (u * g1 + b1).astype(bf16)
     dn = nn(dqkv, w_ref[: 3 * D, :])
     sums = jnp.concatenate([jnp.sum(dn * u, axis=0, keepdims=True), jnp.sum(dn, axis=0, keepdims=True), jnp.zeros((6, D), f32)], axis=0)
-    dx_ref[...] = dx1 + unit_back(u, i1, g1, dn)
+    dx = dx1 + unit_back(u, i1, g1, dn)
+    if first_vec:
+        grad_table = tn(dx.astype(bf16), in_ref[...])
+    else:
+        dx_ref[...] = dx
     last = pl.num_programs(0) - 1
 
     @pl.when(step == 0)
     def _():
-        acc_ref[: 3 * D, :] = tn(dqkv, normed)
-        acc_ref[3 * D :, :] = tn(ab, att_ref[...])
+        acc_ref[...] = tn(dqkv, normed)
+        if first_vec:
+            table_ref[...] = grad_table
         dv_ref[...] = sums
 
     @pl.when(step > 0)
     def _():
-        acc_ref[: 3 * D, :] += tn(dqkv, normed)
-        acc_ref[3 * D :, :] += tn(ab, att_ref[...])
+        acc_ref[...] += tn(dqkv, normed)
+        if first_vec:
+            table_ref[...] += grad_table
         dv_ref[...] += sums
 
     @pl.when(step == last)
     def _():
-        dw_ref[...] = acc_ref[...].astype(bf16)
-
-
-def att_backward(dx1, x, qkv, att, w, layer, gains, seg, step_rows=512):
+        put_halves(core_ref, acc_ref, keep_ref, send_ref)
+        if first_vec:
+            rows, lanes = vec_ref.shape[0], table_ref.shape[1]
+            vec = vec_ref[...] + jnp.concatenate([dv_ref[...], jnp.zeros((rows - 8, D), f32)], axis=0)
+            at = lax.broadcasted_iota(jnp.int32, (rows, lanes), 1) - first_vec
+            pick = (at == lax.broadcasted_iota(jnp.int32, (rows, lanes), 0)).astype(f32).astype(bf16)
+            table_ref[...] += tn(vec.astype(bf16), pick)
+            half = lanes // 2
+            mine = pl.multiple_of(core_ref[0] * half, 128)
+            other = pl.multiple_of((1 - core_ref[0]) * half, 128)
+            tkeep_ref[...] = table_ref[:, pl.ds(mine, half)].astype(bf16)
+            tsend_ref[...] = table_ref[:, pl.ds(other, half)].astype(bf16)
+
+
+def att_backward(core, wide, dx1, x, qkv, w, layer, gains, seg, table=None, step_rows=512):
     rows = x.shape[0]
     steps = rows // step_rows
+    parts = [jax.ShapeDtypeStruct((3 * D // wide, wide // 2, D), bf16)] * 2
+    whole = [whole_spec(p.shape) for p in parts]
+    acc = pltpu.VMEM((3 * D, D), f32)
+    if table is None:
+        first_vec, more, more_specs = 0, (), []
+        out_specs = [rows_spec(step_rows, D), *whole, whole_spec((8, D))]
+        out_shape = [jax.ShapeDtypeStruct((rows, D), f32), *parts, jax.ShapeDtypeStruct((8, D), f32)]
+        scratch = [acc]
+    else:
+        first_vec, inputs, vec = table
+        lanes = inputs.shape[1]
+        more, more_specs = (inputs, vec), [rows_spec(step_rows, lanes), whole_spec(vec.shape)]
+        out_shape = [*parts, *[jax.ShapeDtypeStruct((D, lanes // 2), bf16)] * 2]
+        out_specs = [whole_spec(p.shape) for p in out_shape]
+        scratch = [acc, pltpu.VMEM((8, D), f32), pltpu.VMEM((D, lanes), f32)]
     return pl.pallas_call(
-        att_bwd_kernel,
+        functools.partial(att_bwd_kernel, first_vec),
         grid=(steps,),
         in_specs=[
+            smem_spec(),
             rows_spec(step_rows, D),
             rows_spec(step_rows, D),
             rows_spec(step_rows, 3 * D),
-            rows_spec(step_rows, D),
             third_spec(3 * layer),
             whole_spec(gains.shape),
             rows_spec(step_rows, 1),
             pl.BlockSpec((1, 1, step_rows), lambda i: (i, 0, 0)),
+            *more_specs,
         ],
-        out_specs=[rows_spec(step_rows, D), whole_spec((4 * D, D)), whole_spec((8, D))],
-        out_shape=[jax.ShapeDtypeStruct((rows, D), f32), jax.ShapeDtypeStruct((4 * D, D), bf16), jax.ShapeDtypeStruct((8, D), f32)],
-        scratch_shapes=[pltpu.VMEM((4 * D, D), f32)],
+        out_specs=out_specs,
+        out_shape=out_shape,
+        scratch_shapes=scratch,
         compiler_params=params(),
+        cost_estimate=lasting(18),
         name="att_bwd",
-    )(dx1, x, qkv, att, w, gains, seg[:, None], seg.reshape(steps, 1, step_rows))
+    )(core, dx1, x, qkv, w, gains, seg[:, None], seg.reshape(steps, 1, step_rows), *more)
+
+
+HALF_PI = (1.5703125, 0.000483751296996, 7.54978995489e-08, 5.1266913e-12)
+
+
+def sin_cos(x):
+    k = jnp.round(x * 0.6366197723675814)
+    r = x
+    for part in HALF_PI:
+        r = r - k * part
+    r = jnp.clip(r, -1.0, 1.0)
+    r2 = r * r
+    s = r + r * r2 * (-1.6666654611e-1 + r2 * (8.3321608736e-3 + r2 * -1.9515295891e-4))
+    c = 1.0 - 0.5 * r2 + r2 * r2 * (4.166664568298827e-2 + r2 * (-1.388731625493765e-3 + r2 * 2.443315711809948e-5))
+    n = k.astype(jnp.int32)
+    odd = (n & 1) == 1
+    sin_v = jnp.where(odd, c, s)
+    cos_v = jnp.where(odd, s, c)
+    sin_v = jnp.where((n & 2) == 2, -sin_v, sin_v)
+    cos_v = jnp.where(((n + 1) & 2) == 2, -cos_v, cos_v)
+    return sin_v, cos_v
+
+
+def head_kernel(several, s_ref, all_ref, rff_ref, read_ref, w_ref, gread_ref, grff_ref, sums_ref, sin_ref, cos_ref):
+    features = all_ref[:, :D]
+    logits = all_ref[:, D:]
+    phases = nn(features, rff_ref[...])
+    large = jnp.max(jnp.abs(phases)) > 5e4
+
+    @pl.when(large)
+    def _():
+        sin_ref[...] = jnp.sin(phases)
+        cos_ref[...] = jnp.cos(phases)
+
+    @pl.when(jnp.logical_not(large))
+    def _():
+        sin_ref[...], cos_ref[...] = sin_cos(phases)
+
+    lifted = cos_ref[...].astype(bf16)
+    back = (-sin_ref[...] * nn(logits, read_ref[...])).astype(bf16)
+    blocks = pl.num_programs(1)
+    gread = tn(logits, lifted)
+    grff = tn(features, back)
+    if several:
+        block = pl.program_id(1)
+
+        @pl.when(block == 0)
+        def _():
+            gread_ref[...] = gread
+            grff_ref[...] = grff
+
+        @pl.when(block > 0)
+        def _():
+            gread_ref[...] += gread
+            grff_ref[...] += grff
+
+        @pl.when(block == blocks - 1)
+        def _():
+            head_finish(s_ref, w_ref, gread_ref[...], grff_ref[...], gread_ref, grff_ref, sums_ref)
+    else:
+        head_finish(s_ref, w_ref, gread, grff, gread_ref, grff_ref, sums_ref)
+
+
+def head_finish(s_ref, w_ref, gread, grff, gread_ref, grff_ref, sums_ref):
+    step = pl.program_id(0)
+    w = w_ref[...]
+    gread = gread * s_ref[0] + 2.0 * l2_weight * w
+    grff = grff * s_ref[0]
+    gread_ref[...] = gread
+    grff_ref[...] = grff
+    total = jnp.sum(jnp.sum(gread * gread, axis=0, keepdims=True)) + jnp.sum(jnp.sum(grff * grff, axis=0, keepdims=True))
+    ridge = jnp.sum(jnp.sum(w * w, axis=0, keepdims=True))
+    row = lax.broadcasted_iota(jnp.int32, (8, 128), 0)
+    tile = jnp.where(row == 0, total, jnp.where(row == 1, ridge, 0.0))
+
+    @pl.when(step == 0)
+    def _():
+        sums_ref[...] = tile
+
+    @pl.when(step > 0)
+    def _():
+        sums_ref[...] += tile
+
+
+def head_backward(scale, every, rff, read, w, cols=256):
+    n, classes = every.shape[0], read.shape[0]
+    width = rff.shape[1]
+    cols = min(cols, width)
+    rows = math.gcd(n, 768)
+    col = lambda r: pl.BlockSpec((r, cols), lambda i, j: (0, i))
+    return pl.pallas_call(
+        functools.partial(head_kernel, n > rows),
+        grid=(width // cols, n // rows),
+        in_specs=[smem_spec(), pl.BlockSpec((rows, every.shape[1]), lambda i, j: (j, 0)), col(D), col(classes), col(classes)],
+        out_specs=[col(classes), col(D), whole_spec((8, 128))],
+        out_shape=[jax.ShapeDtypeStruct((classes, width), f32), jax.ShapeDtypeStruct((D, width), f32), jax.ShapeDtypeStruct((8, 128), f32)],
+        scratch_shapes=[pltpu.VMEM((rows, cols), f32)] * 2,
+        compiler_params=params(56, 2),
+        cost_estimate=lasting(12),
+        name="head_bwd",
+    )(scale, every, rff, read, w)
 
 
 POS = 197
@@ -464,56 +629,68 @@
 rate_matrix = 0.05
 rate_vector = 0.5
 ema_rate = 0.5
-ALL = ("dp", "narrow")
+DP = ("dph", "dpl")
+NARROW = ("ny", "nc")
+ALL = DP + NARROW
+
+
+def swap(rows, axis, mask):
+    return lax.ppermute(rows, axis, [(i, i ^ mask) for i in range(lax.axis_size(axis))])
+
+
+def add_up(terms):
+    return sum(t.astype(f32) for t in terms)
 
 
 def bits_of(size):
     return size.bit_length() - 1
 
 
-def swap(rows, axis, mask):
-    return lax.ppermute(rows, axis, [(i, i ^ mask) for i in range(lax.axis_size(axis))])
-
-
-def add_low(left, right):
-    return (left.astype(f32) + right.astype(f32)).astype(bf16)
-
-
-def halve(rows, dim, axis, bit):
-    half = rows.shape[dim] // 2
-    mine = (lax.axis_index(axis) >> bit) & 1
-    keep = lax.dynamic_slice_in_dim(rows, mine * half, half, dim)
-    send = lax.dynamic_slice_in_dim(rows, (1 - mine) * half, half, dim)
-    return add_low(keep, swap(send, axis, 1 << bit))
-
-
-def sum_narrow(rows, dim):
-    for bit in range(bits_of(lax.axis_size("narrow"))):
-        rows = halve(rows, dim, "narrow", bit)
-    return rows
-
-
-def sum_dp(rows):
-    for bit in range(bits_of(lax.axis_size("dp"))):
-        rows = rows.reshape(rows.shape[0] // 2, 2, *rows.shape[1:])
-        rows = halve(rows, 1, "dp", bit)
-        rows = rows.reshape(rows.shape[0], *rows.shape[2:])
-    return rows[0]
+class Slab:
+    def __init__(self, terms):
+        self.terms = terms
+
+    def hop(self, dim, axis, bit=0):
+        half = self.terms[0].shape[dim] // 2
+        mine = (lax.axis_index(axis) >> bit) & 1
+        send = add_up([lax.dynamic_slice_in_dim(t, (1 - mine) * half, half, dim) for t in self.terms])
+        self.terms = [lax.dynamic_slice_in_dim(t, mine * half, half, dim) for t in self.terms]
+        return swap(send.astype(bf16), axis, 1 << bit)
+
+    def hops_y(self, dim):
+        bits = bits_of(lax.axis_size("ny"))
+        for bit in range(bits - 1):
+            self.terms.append(self.hop(dim, "ny", bit))
+        return self.hop(dim, "ny", bits - 1)
+
+    def hop_x(self):
+        self.terms = [t.reshape(t.shape[0] // 2, 2, *t.shape[1:]) for t in self.terms]
+        got = self.hop(1, "dpl")
+        self.terms = [t.reshape(t.shape[0], *t.shape[2:]) for t in self.terms]
+        return got.reshape(got.shape[0], *got.shape[2:])
+
+    def low(self):
+        return add_up(self.terms).astype(bf16)
+
+
+def spread(rows):
+    return lax.all_to_all(rows, "dph", 0, 0)
 
 
 def join_narrow(piece):
-    every = lax.all_gather(piece, "narrow", axis=0, tiled=False)
-    size = every.shape[0]
-    bits = bits_of(size)
-    order = [int(format(i, "b").zfill(bits)[::-1], 2) for i in range(size)]
-    return [every[i] for i in order]
+    every = lax.all_gather(piece, NARROW, axis=0, tiled=False)
+    cores, ys = lax.axis_size("nc"), lax.axis_size("ny")
+    bits = bits_of(ys)
+    flip = [int(format(i, "b").zfill(bits)[::-1], 2) for i in range(ys)]
+    return [every[flip[y] * cores + core] for core in range(cores) for y in range(ys)]
 
 
 def total_of(scalars):
+    lane = lax.broadcasted_iota(jnp.int32, (8, 128), 1)
     tile = jnp.zeros((8, 128), f32)
     for i, value in enumerate(scalars):
-        tile = tile.at[0, i].set(value)
-    world = lax.axis_size("dp") * lax.axis_size("narrow")
+        tile = jnp.where(lane == i, value, tile)
+    world = lax.axis_size(ALL)
     every = lax.all_to_all(jnp.broadcast_to(tile[None], (world, 8, 128)), ALL, 0, 0)
     row = jnp.sum(every, axis=0)[0]
     return [row[i] for i in range(len(scalars))]
@@ -561,12 +738,11 @@
     read_v,
     read_e,
 ):
-    n_dp, n_narrow = lax.axis_size("dp"), lax.axis_size("narrow")
-    me_dp, me_narrow = lax.axis_index("dp"), lax.axis_index("narrow")
+    n_dp, n_narrow = lax.axis_size(DP), lax.axis_size(NARROW)
+    me_dp, me_narrow = lax.axis_index(DP), lax.axis_index(NARROW)
     own_dim = embed_w.shape[1]
     own_wide = mats_w.shape[2]
-    group = math.gcd(own_wide, PART)
-    groups = WIDE // group
+    core = lax.axis_index("nc").astype(jnp.int32).reshape(1)
     slots = cls_row.shape[0]
     table_rows = -(-(embed_w.shape[0] + vector_w.shape[0]) // 256) * 256
     chunk = table_rows // n_narrow
@@ -574,7 +750,7 @@
     image_total = total_of([jnp.sum(img_count).astype(f32)])[0]
     slot_ids = jnp.arange(slots)
     valid = (slot_ids % IMG_SEQ < jnp.repeat(img_count, IMG_SEQ, total_repeat_length=slots)).astype(jnp.int32)
-    facts = lax.all_gather(jnp.stack([labels, valid]), "narrow", axis=0)
+    facts = lax.all_gather(jnp.stack([labels, valid]), NARROW, axis=0)
     group_labels = facts[:, 0].reshape(-1)
     group_valid = facts[:, 1].reshape(-1).astype(f32)[:, None]
 
@@ -604,65 +780,90 @@
 
     rff_low = rff_w.astype(bf16)
     read_low = read_w.T.astype(bf16)
-    group_rows = lax.all_gather(features, "narrow", axis=0, tiled=True)
+    group_rows = lax.all_gather(features, NARROW, axis=0, tiled=True)
     phases = nn(group_rows, rff_low)
     lifted = jnp.cos(phases).astype(bf16)
-    partial = lax.all_gather(nt(lifted, read_low).astype(bf16), "narrow", axis=0)
+    partial = lax.all_gather(nt(lifted, read_low).astype(bf16), NARROW, axis=0)
     logits = jnp.sum(partial.astype(f32), axis=0)
     error = logits - (group_labels[:, None] == jnp.arange(CLASSES)[None, :]).astype(f32)
     error_sum = jnp.sum(group_valid * error * error)
     grad_logits = (2.0 * group_valid * error).astype(bf16)
     grad_phases = (-jnp.sin(phases) * nn(grad_logits, read_low)).astype(bf16)
     grad_pieces = nt(grad_phases, rff_low).reshape(n_narrow, slots, D)
-    grad_features = jnp.sum(lax.all_to_all(grad_pieces, "narrow", 0, 0), axis=0)
+    grad_features = jnp.sum(lax.all_to_all(grad_pieces, NARROW, 0, 0), axis=0)
     grad_features = jnp.pad(grad_features, ((0, pad), (0, 0)))
 
     own_logits = lax.dynamic_slice_in_dim(grad_logits, me_narrow * slots, slots, 0)
     every = lax.all_gather(jnp.concatenate([features, own_logits], axis=1), ALL, axis=0, tiled=True)
-    all_features, all_logits = every[:, :D], every[:, D:]
-    all_phases = nn(all_features, rff_low)
-    all_lifted = jnp.cos(all_phases).astype(bf16)
-    all_grad = (-jnp.sin(all_phases) * nn(all_logits, read_low)).astype(bf16)
-    grad_read = tn(all_logits, all_lifted).T
-    grad_rff = tn(all_features, all_grad)
-
-    xs, cls_kept = x1, kept[:-1]
-    grad_state, grad_last, vec_last = last_backward(cls, grad_features, xs, mats, L - 1, last_gains, segments, seg_cls, *cls_kept)
-    sums = [None] * L
-    sums[L - 1] = sum_dp(sum_narrow(grad_last.reshape(groups, group, D), 1).reshape(n_dp, -1, D))
-    vecs = [vec_last[:6]]
+    scale = 1.0 / image_total
+
+    tie = lax.optimization_barrier
+    state, keep, send, vec = last_backward(cls, core, own_wide, grad_features, x1, mats, L - 1, last_gains, segments, seg_cls, *kept[:-1])
+    vecs = [vec[:6]]
+    whole = Slab([keep])
+    done = {}
+    flight = {(L - 1, "c"): (whole, swap(send, "nc", 1))}
+    parts = {}
+
+    def land(outs):
+        keys = list(flight)
+        outs, got = tie((outs, [flight[k][1] for k in keys]))
+        for (name, at), g in zip(keys, got):
+            slab = flight.pop((name, at))[0]
+            slab.terms.append(g)
+            if at == "c":
+                flight[(name, "y")] = (slab, slab.hops_y(2 if name == "table" else 1))
+            elif at == "y":
+                flight[(name, "x")] = (slab, slab.hop_x())
+            else:
+                parts[name] = slab.low()
+                if name == L - 1:
+                    done[name] = spread(parts[name])
+                elif name == (1, "a"):
+                    done[1] = spread(jnp.concatenate([parts[(1, "a")], parts[(1, "m")]]))
+        return outs
+
     for layer in reversed(range(L - 1)):
         x, qkv, att, mid = states[layer]
         lg = gains[4 * layer : 4 * layer + 4]
-        grad_mid, grad_mlp, vec_mlp = mlp_backward(grad_state, mid, mats, layer, lg)
-        mlp_sum = sum_narrow(grad_mlp.reshape(-1, group, D), 1)
-        grad_state, grad_att, vec_att = att_backward(grad_mid, x, qkv, att, mats, layer, lg, segments)
-        att_sum = sum_narrow(grad_att.reshape(-1, group, D), 1)
-        sums[layer] = sum_dp(jnp.concatenate([att_sum, mlp_sum]).reshape(n_dp, -1, D))
-        vecs = [vec_att[:2], vec_mlp[:2]] + vecs
-    vec = jnp.concatenate(vecs).T
-    grad_table = tn(grad_state.astype(bf16), inputs)
-    grad_table = grad_table + jnp.pad(vec, ((0, 0), (first_vec, table_rows - first_vec - vec.shape[1])))
-    table_sum = sum_narrow(grad_table.astype(bf16), 1).reshape(n_dp, own_dim, chunk)
-    table_sum = sum_dp(table_sum)
-
-    scale = 1.0 / image_total
-    read_step = grad_read * scale + 2.0 * l2_weight * read_w
-    rff_step = grad_rff * scale
+        outs = mlp_backward(core, own_wide, state, mid, att, mats, layer, lg)
+        grad_mid, keep, send, vec_mlp = land(outs)
+        flight[((layer, "m"), "c")] = (Slab([keep]), swap(send, "nc", 1))
+        if layer:
+            outs = att_backward(core, own_wide, grad_mid, x, qkv, mats, layer, lg, segments)
+            state, keep, send, vec_att = land(outs)
+            vecs = [vec_att[:2], vec_mlp[:2]] + vecs
+        else:
+            vec = jnp.concatenate([jnp.zeros((2, D), f32), vec_mlp[:2]] + vecs)
+            vec = jnp.pad(vec, ((0, -vec.shape[0] % 16), (0, 0)))
+            outs = att_backward(core, own_wide, grad_mid, x, qkv, mats, layer, lg, segments, (first_vec, inputs, vec))
+            keep, send, tkeep, tsend = land(outs)
+            tkeep = tkeep.reshape(n_dp, own_dim, -1)
+            flight[("table", "c")] = (Slab([tkeep]), swap(tsend.reshape(tkeep.shape), "nc", 1))
+        flight[((layer, "a"), "c")] = (Slab([keep]), swap(send, "nc", 1))
+    read_step, rff_step, head_sums = land(head_backward(scale.reshape(1), every, rff_low, read_low, read_w.T))
+    while flight:
+        land(())
+    side = parts["table"].reshape(n_dp // 2, -1, D)
+    both = spread(jnp.concatenate([jnp.concatenate([parts[(0, "a")], parts[(0, "m")]]), side], axis=1))
+    cut = own_wide // n_narrow
+    sums = jnp.concatenate([add_up(list(both)), *(add_up(list(done[i])) for i in range(1, L))])
+
     first_dp = (me_dp == 0).astype(f32)
     first_narrow = (me_narrow == 0).astype(f32)
-    local = square_sum([*sums, table_sum]) * (scale * scale)
-    local = local + first_dp * square_sum([read_step, rff_step])
-    ridge = first_dp * jnp.sum(read_w * read_w)
+    local = square_sum([sums]) * (scale * scale)
+    local = local + first_dp * head_sums[0, 0]
+    ridge = first_dp * head_sums[1, 0]
     total_square, error_total, ridge_total = total_of([local, first_narrow * error_sum, ridge])
     loss_sum = error_total + l2_weight * image_total * ridge_total
     clip_norm = jnp.sqrt(total_square)
     factor = jnp.minimum(1.0, clip_bound / clip_norm)
 
-    rows = jnp.stack([s.reshape(-1, group // n_narrow, D) for s in sums])
-    rows = jnp.stack(join_narrow(rows), axis=2).reshape(L, own_wide, D)
+    shares = join_narrow(sums.astype(bf16))
+    starts = [0, cut + side.shape[1], 2 * cut + side.shape[1]]
+    rows = jnp.stack([jnp.concatenate([s[a : a + cut] for s in shares]) for a in starts])
     grad_mats = jnp.swapaxes(rows, 1, 2).astype(f32) * scale
-    lanes = jnp.concatenate(join_narrow(table_sum), axis=1).astype(f32) * scale
+    lanes = jnp.concatenate([s[cut : starts[1]].reshape(own_dim, chunk) for s in shares], axis=1).astype(f32) * scale
     grad_embed = lanes[:, :first_vec].T
     grad_vector = lanes[:, first_vec : first_vec + vector_w.shape[0]].T
 
@@ -671,13 +872,15 @@
     outs += adamw(vector_w, vector_m, vector_v, vector_e, grad_vector * factor, rate_vector, 0.0)
     outs += adamw(mats_w, mats_m, mats_v, mats_e, grad_mats * factor, rate_matrix, weight_decay)
     outs += adamw(rff_w, rff_m, rff_v, rff_e, rff_step * factor, rate_matrix, weight_decay)
-    outs += adamw(read_w, read_m, read_v, read_e, read_step * factor, rate_matrix, weight_decay)
+    outs += adamw(read_w, read_m, read_v, read_e, read_step.T * factor, rate_matrix, weight_decay)
     return tuple(outs)
 
 
 def solution(mesh):
+    n_dp, n_narrow = mesh.shape["dp"], mesh.shape["narrow"]
+    fine = jax.sharding.Mesh(mesh.devices.reshape(n_dp // 2, 2, n_narrow // 2, 2), ALL)
     rows = P(ALL)
-    table, mats, rff, read = P(None, "dp"), P(None, None, "dp"), P(None, "narrow"), P("narrow", None)
+    table, mats, rff, read = P(None, DP), P(None, None, DP), P(None, NARROW), P(NARROW, None)
     ins = (P(ALL, None),) + (rows,) * 5 + (table,) * 8 + (mats,) * 4 + (rff,) * 4 + (read,) * 4
     outs = (P(),) * 3 + (table,) * 10 + (mats,) * 5 + (rff,) * 5 + (read,) * 5
-    return jax.shard_map(shards, mesh=mesh, in_specs=ins, out_specs=outs, check_vma=False)
+    return jax.shard_map(shards, mesh=fine, in_specs=ins, out_specs=outs, check_vma=False)

time: 506 us -> 435 us (0.86)
  matrix products: 45.4 us -> 4.53 us
  waiting for transfers between devices: 79 us -> 51.2 us
  Pallas kernels: 127 us -> 147 us
  local copies, waits for them, and re-layouts: 50.6 us -> 40.6 us
  blocking collectives: 70.5 us -> 64.5 us
    ppermute x24 -> x18, waiting for transfers between devices: 60.4 us -> 14.9 us  [swap(): lax.ppermute(rows, axis, [(i, i ^ mask) for i in range(lax.axis_size(axis...]
    dot_general x3 -> x0, matrix products: 36.6 us -> none  [tn(): lax.dot_general(a, b, (((0,), (0,)), ((), ())), preferred_element_type=f32)]
    pallas_call x5 -> x6, Pallas kernels: 83.4 us -> 103 us  [the longest x2 37.7 us: att_backward(): pl.pallas_call(functools.partial(att_bwd_kernel, first_vec), grid=(steps,...]
    all_to_all x1 -> x4, waiting for transfers between devices: 2.92 us -> 19.8 us  [the longest x3 15.6 us: spread(): return lax.all_to_all(rows, 'dph', 0, 0)]
    all_to_all x1 -> x4, starting transfers between devices: 3.34 us -> 15.9 us  [the longest x3 12.6 us: spread(): return lax.all_to_all(rows, 'dph', 0, 0)]
    ppermute x24 -> x18, starting transfers between devices: 25.2 us -> 13.2 us  [swap(): lax.ppermute(rows, axis, [(i, i ^ mask) for i in range(lax.axis_size(axis...]
    all_gather x4 -> x3, blocking collectives: 25.1 us -> 19.1 us  [the longest x1 8.71 us: shards(): partial = lax.all_gather(nt(lifted, read_low).astype(bf16), NARROW, axis=0)]
    all_gather x1, waiting for transfers between devices: 8.25 us -> 13.7 us  [shards(): lax.all_gather(mats_own.astype(bf16), ALL, axis=1, tiled=True)]
  transfers between devices with their start and end apart: 30 -> 27, of which waited for: 14 -> 9; matrix products, arithmetic and copies ran while one was open for 17% -> 16% of each run, Pallas kernels for 17% -> 20%
where the time goes in v2:
time: 435 us; the launch traced here: 431 us
  Pallas kernels  147 us (34%)
  blocking collectives  64.5 us (15%)
  other arithmetic  58.7 us (13%)
  waiting for transfers between devices  51.2 us (12%)
  local copies, waits for them, and re-layouts  40.6 us (9%)
  starting transfers between devices  39.9 us (9%)
  between operations  23.9 us (5%)
  matrix products  4.53 us (1%)
    all_gather x1, blocking collectives, shards(): table = lax.all_gather(table, ALL, axis=0)  45.5 us
    pallas_call x2, Pallas kernels, att_backward(): pl.pallas_call(functools.partial(att_bwd_kernel, first_vec), grid=(steps,...  37.7 us
    pallas_call x2, Pallas kernels, mlp_backward(): pl.pallas_call(mlp_bwd_kernel, grid=(steps,), in_specs=[smem_spec(), *[ro...  33.2 us
    convert_element_type x5, other arithmetic, adamw(): return (weight, first, second, average, weight.astype(bf16))  20.9 us
    pallas_call x1, Pallas kernels, first_forward(): pl.pallas_call(first_kernel, grid=(steps,), in_specs=[rows_spec(step_rows...  17.9 us
    pallas_call x1, Pallas kernels, head_backward(): pl.pallas_call(functools.partial(head_kernel, n > rows), grid=(width // c...  17.3 us
    pallas_call x1, Pallas kernels, layer_forward(): pl.pallas_call(fwd_kernel, grid=(steps,), in_specs=[rows_spec(step_rows,...  17.3 us
    unnamed x123, local copies, waits for them, and re-layouts  17 us
  transfers between devices with their start and end apart: 27, of which 9 were waited for; matrix products, arithmetic and copies ran while one was open for 16% of the time, Pallas kernels for 20%

profile of v2, /device:TPU:0, one launch (start us, length us, event | category | flops | bytes accessed | tf_op | source)
XLA Modules:
  0.0 430.6 jit_solution(13774695567068156362)
XLA Ops:
  7.3 1.9 fusion.14
  11.8 7.3 %all-to-all-start = ((f32[32,8,128]{2,1,0:T(8,128)}), f32[32,8,128]{2,1,0:T(8,128)S(1)}, u32[]{:S(2)}, u32[]{:S(2)}) async-start(f32[32,8,128]{2,1,0:T(8,128)} %broadcast_in_dim.59), calls=%async_computation | async-start | bytes 262144 | tf_op jit(solution)/shard_map/all_to_all | solution.py:694
  22.2 45.5 %all-gather = bf16[1536,256]{1,0:T(8,128)(2,1)S(1)} all-gather(bf16[48,256]{1,0:T(8,128)(2,1)S(1)} %fusion.20), channel_id=2, replica_groups=mesh['dph'=4,'dpl'=2,'ny'=2,'nc'=2] {'dph','dpl','ny','nc'}, dimensions={0}, use_global_device_ids=true | all-gather | bytes 811008 | tf_op jit(solution)/shard_map/all_gather | solution.py:760
  70.0 2.6 compare_convert_fusion
  72.6 5.1 %all-gather.3 = s32[4,2,24]{2,1,0:T(2,128)S(1)} all-gather(s32[1,2,24]{2,1,0:T(2,128)S(1)} %add_bitcast_fusion), channel_id=3, replica_groups=mesh['dph'=4,'dpl'=2,'ny'=2,'nc'=2] {'ny','nc'}, dimensions={0}, use_global_device_ids=true | all-gather | bytes 960 | tf_op jit(solution)/shard_map/all_gather | solution.py:753
  78.5 2.5 bitcast_convert_fusion.read_ref
  82.3 1.5 convert_element_type.485.rff_ref
  89.8 13.7 %all-gather.8.cloned.1.call-done = bf16[3,4608,384]{2,1,0:T(8,128)(2,1)} async-done(((bf16[3,144,384]{2,1,0:T(8,128)(2,1)}), bf16[3,4608,384]{2,1,0:T(8,128)(2,1)}) %all-gather.8.cloned.1.call-update) | async-done | bytes 10616848 | tf_op jit(solution)/shard_map/all_gather | solution.py:764
  103.5 17.9 %first_fwd.1 = (bf16[1024,1024]{1,0:T(8,128)(2,1)}, f32[1024,384]{1,0:T(8,128)}, bf16[1024,1152]{1,0:T(8,128)(2,1)}, bf16[1024,384]{1,0:T(8,128)(2,1)}, f32[1024,384]{1,0:T(8,128)}, /*index=5*/f32[1024,384]{1,0:T(8,128)}) custom-call(bf16[1024,768]{1,0:T(8,128)(2,1)} %p_ref.1, s32[1024,1]{1,0:T(8,128)} %copy.220.pos_ref, bf16[384,1024]{1,0:T(8,128)(2,1)} %bitcast.217, ...), custom_call_target="tpu_custom_call" | custom-call | flops 17999998976 | bytes 36000000 | tf_op jit(solution)/shard_map/first_fwd/pallas_call | solution.py:170
  121.5 17.3 %layer_fwd.1 = (bf16[1024,1152]{1,0:T(8,128)(2,1)}, bf16[1024,384]{1,0:T(8,128)(2,1)}, f32[1024,384]{1,0:T(8,128)}, f32[1024,384]{1,0:T(8,128)}) custom-call(f32[1024,384]{1,0:T(8,128)} %get-tuple-element.117.x_ref.refs_2_, bf16[13824,384]{1,0:T(8,128)(2,1)} %bitcast.178, bf16[13824,384]{1,0:T(8,128)(2,1)} %bitcast.179, bf16[13824,384]{1,0:T(8,128)(2,1)} %bitcast.180, ...), custom_call_target="tpu_custom_call" | custom-call | flops 16999999488 | bytes 34000000 | tf_op jit(solution)/shard_map/layer_fwd/pallas_call | solution.py:143
  138.8 8.6 %last_fwd.1 = (bf16[1024,768]{1,0:T(8,128)(2,1)}, f32[32,384]{1,0:T(8,128)}, bf16[32,384]{1,0:T(8,128)(2,1)}, bf16[32,384]{1,0:T(8,128)(2,1)}, f32[32,384]{1,0:T...) custom-call(s32[32]{0:T(128)} %concatenate.51.cls_ref, f32[1024,384]{1,0:T(8,128)} %get-tuple-element.118.x_ref, ...), custom_call_target="tpu_custom_call" | custom-call | flops 8999999488 | bytes 18000000 | tf_op jit(solution)/shard_map/last_fwd/pallas_call | solution.py:251
  148.1 5.3 %all_gather.36 = bf16[96,384]{1,0:T(8,128)(2,1)S(1)} all-gather(bf16[24,384]{1,0:T(8,128)(2,1)S(1)} %slice.199), channel_id=1, replica_groups=mesh['dph'=4,'dpl'=2,'ny'=2,'nc'=2] {'ny','nc'}, dimensions={0}, use_global_device_ids=true | all-gather | bytes 92160 | tf_op jit(solution)/shard_map/all_gather | solution.py:783
  153.7 1.7 convolution_convert_fusion
  155.4 8.7 %all-gather.2 = bf16[384,1000]{1,0:T(8,128)(2,1)S(1)} all-gather(bf16[96,1000]{1,0:T(8,128)(2,1)S(1)} %convolution_convert_fusion), channel_id=4, replica_groups=mesh['dph'=4,'dpl'=2,'ny'=2,'nc'=2] {'ny','nc'}, dimensions={0}, use_global_device_ids=true | all-gather | bytes 960000 | tf_op jit(solution)/shard_map/all_gather | solution.py:786
  165.1 2.5 fusion.4
  167.6 3.3 all-to-all-start.1
  171.5 4.2 all-to-all-done.1
  176.4 15.1 %last_bwd.1 = (f32[1024,384]{1,0:T(8,128)}, bf16[8,288,384]{2,1,0:T(8,128)(2,1)}, bf16[8,288,384]{2,1,0:T(8,128)(2,1)}, f32[8,384]{1,0:T(8,128)}) custom-call(s32[32]{0:T(128)} %concatenate.51.cls_ref, s32[1]{0:T(128)} %bitcast.24.core_ref.refs_0_, f32[32,384]{1,0:T(8,128)} %pad.17.df_ref, f32[1024,384]{1,0:T(8,128)} %get-tuple-element.118.x_ref, ...), custom_call_target="tpu_custom_call" | custom-call | flops 15000000512 | bytes 30000000 | tf_op jit(solution)/shard_map/last_bwd/pallas_call | solution.py:332
  193.5 16.6 %mlp_bwd.2 = (f32[1024,384]{1,0:T(8,128)}, bf16[6,288,384]{2,1,0:T(8,128)(2,1)}, bf16[6,288,384]{2,1,0:T(8,128)(2,1)}, f32[8,384]{1,0:T(8,128)}) custom-call(s32[1]{0:T(128)} %bitcast.24.core_ref.refs_0_, f32[1024,384]{1,0:T(8,128)} %get-tuple-element.129.dxo_ref, f32[1024,384]{1,0:T(8,128)} %get-tuple-element.130.x1_ref, ...), custom_call_target="tpu_custom_call" | custom-call | flops 16000000000 | bytes 32000000 | tf_op jit(solution)/shard_map/mlp_bwd/pallas_call | solution.py:388
  211.0 17.9 %att_bwd.2 = (f32[1024,384]{1,0:T(8,128)}, bf16[2,288,384]{2,1,0:T(8,128)(2,1)}, bf16[2,288,384]{2,1,0:T(8,128)(2,1)}, f32[8,384]{1,0:T(8,128)}) custom-call(s32[1]{0:T(128)} %bitcast.24.core_ref.refs_0_, f32[1024,384]{1,0:T(8,128)} %get-tuple-element.137.refs_1_, f32[1024,384]{1,0:T(8,128)} %get-tuple-element.117.x_ref.refs_2_, ...), custom_call_target="tpu_custom_call" | custom-call | flops 17999998976 | bytes 36000000 | tf_op jit(solution)/shard_map/att_bwd/pallas_call | solution.py:492
  229.8 3.8 collective-permute-done.1
  237.0 16.6 %mlp_bwd.3 = (f32[1024,384]{1,0:T(8,128)}, bf16[6,288,384]{2,1,0:T(8,128)(2,1)}, bf16[6,288,384]{2,1,0:T(8,128)(2,1)}, f32[8,384]{1,0:T(8,128)}) custom-call(s32[1]{0:T(128)} %bitcast.24.core_ref.refs_0_, f32[1024,384]{1,0:T(8,128)} %get-tuple-element.147.dxo_ref, f32[1024,384]{1,0:T(8,128)} %get-tuple-element.148.x1_ref, ...), custom_call_target="tpu_custom_call" | custom-call | flops 16000000000 | bytes 32000000 | tf_op jit(solution)/shard_map/mlp_bwd/pallas_call | solution.py:388
  255.1 2.1 fusion.5
  257.2 3.9 all-to-all-start.4
  264.1 1.7 collective-permute-start.7
  265.8 19.8 %att_bwd.3 = (bf16[2,288,384]{2,1,0:T(8,128)(2,1)}, bf16[2,288,384]{2,1,0:T(8,128)(2,1)}, bf16[384,512]{1,0:T(8,128)(2,1)}, bf16[384,512]{1,0:T(8,128)(2,1)}) custom-call(s32[1]{0:T(128)} %bitcast.24.core_ref.refs_0_, f32[1024,384]{1,0:T(8,128)} %get-tuple-element.159.refs_1_, f32[1024,384]{1,0:T(8,128)} %get-tuple-element.160.refs_2_, ...), custom_call_target="tpu_custom_call" | custom-call | flops 17999998976 | bytes 36000000 | tf_op jit(solution)/shard_map/att_bwd/pallas_call | solution.py:492
  287.6 17.3 %head_bwd.1 = (f32[1000,1024]{1,0:T(8,128)}, f32[384,1024]{1,0:T(8,128)}, f32[8,128]{1,0:T(8,128)}) custom-call(f32[1]{0:T(128)} %bitcast.1.s_ref, bf16[768,1384]{1,0:T(8,128)(2,1)} %all-gather.10.cloned.1.call-done.all_ref, bf16[384,1024]{1,0:T(8,128)(2,1)} %copy-done.5, bf16[1000,1024]{1,0:T(8,128)(2,1)} %copy-done.1, f32[1000,1024]{1,0:T(8,128)} %bitcast.200), custom_call_target="tpu_custom_call" | custom-call | flops 12000000000 | bytes 24000000 | tf_op jit(solution)/shard_map/head_bwd/pallas_call | solution.py:603
  308.3 3.6 collective-permute-done.9
  314.6 1.6 collective-permute-start.14
  317.8 4.7 %collective-permute-done.14 = bf16[8,48,256]{2,1,0:T(8,128)(2,1)S(1)} collective-permute-done((bf16[8,48,256]{2,1,0:T(8,128)(2,1)S(1)}, bf16[8,48,256]{2,1,0:T(8,128)(2,1)S(1)}, u32[]{:S(2)}, u32[]{:S(2)}) %collective-permute-start.14) | collective-permute-done | bytes 196640 | tf_op jit(solution)/shard_map/ppermute | solution.py:638
  322.5 2.8 collective-permute-done.15
  328.3 5.2 %all-to-all-start.3 = ((bf16[4,144,384]{2,1,0:T(8,128)(2,1)}), bf16[4,144,384]{2,1,0:T(8,128)(2,1)S(1)}, u32[]{:S(2)}, u32[]{:S(2)}) async-start(bf16[4,144,384]{2,1,0:T(8,128)(2,1)} %pad_maximum_fusion.2), calls=%async_computation.3 | async-start | bytes 884736 | tf_op jit(solution)/shard_map/all_to_all | solution.py:677
  337.8 6.3 %all-to-all-done.3 = bf16[4,144,384]{2,1,0:T(8,128)(2,1)S(1)} async-done(((bf16[4,144,384]{2,1,0:T(8,128)(2,1)}), bf16[4,144,384]{2,1,0:T(8,128)(2,1)S(1)}, u32[]{:S(2)}, u32[]{:S(2)}) %all-to-all-start.3) | async-done | bytes 442400 | tf_op jit(solution)/shard_map/all_to_all | solution.py:677
  344.1 3.5 all-to-all-start.2
  351.1 9.3 %all-to-all-done.2 = bf16[4,176,384]{2,1,0:T(8,128)(2,1)S(1)} async-done(((bf16[4,176,384]{2,1,0:T(8,128)(2,1)}), bf16[4,176,384]{2,1,0:T(8,128)(2,1)S(1)}, u32[]{:S(2)}, u32[]{:S(2)}) %all-to-all-start.2) | async-done | bytes 540704 | tf_op jit(solution)/shard_map/all_to_all | solution.py:677
  362.5 2.8 all-to-all-start.5
  370.9 2.8 all-to-all-done.5
  375.0 5.3 %fusion.32 = (bf16[384,1024]{1,0:T(8,128)(2,1)}, f32[384,1024]{1,0:T(8,128)S(1)}, f32[384,1024]{1,0:T(8,128)}, f32[384,1024]{1,0:T(8,128)}) fusion(f32[384,1024]{1,0:T(8,128)S(1)} %copy-done.6, f32[384,1024]{1,0:T(8,128)} %get-tuple-element.192, f32[]{:T(128)S(6)} %min.3, f32[384,1024]{1,0:T(8,128)} %param.47, f32[384,1024]{1,0:T(8,128)} %param.48), kind=kLoop, calls=%fused_computation.137 | loop fusion | flops 6291456 | bytes 11796484 | tf_op jit(solution)/shard_map/convert_element_type | solution.py:706
  381.7 3.0 add_multiply_fusion.2
  384.7 9.1 %fusion.30 = (bf16[1024,1000]{0,1:T(8,128)(2,1)}, f32[1024,1000]{0,1:T(8,128)S(1)}, f32[1024,1000]{0,1:T(8,128)}, f32[1024,1000]{0,1:T(8,128)}) fusion(f32[1024,1000]{0,1:T(8,128)S(1)} %copy-done.3, f32[1000,1024]{1,0:T(8,128)} %get-tuple-element.193, f32[]{:T(128)S(6)} %min.3, f32[1024,1000]{0,1:T(8,128)} %param.51, f32[1024,1000]{0,1:T(8,128)} %param.52), kind=kLoop, calls=%fused_computation.136 | loop fusion | flops 16384000 | bytes 30720004 | tf_op jit(solution)/shard_map/convert_element_type | solution.py:706
  393.8 2.0 copy-done.2
  395.8 2.9 add_multiply_fusion
  403.7 2.0 copy.247
  405.8 1.9 add_multiply_fusion.3
  407.6 1.9 copy.248
  412.3 1.6 slice_bitcast_fusion.11
  415.3 3.9 fusion.34
  419.2 2.0 add_multiply_fusion.1
  (256 shorter events, 64.0 us)
Async XLA Ops:
  7.2 96.3 %all-gather.8.cloned.1.call-start = ((), (), s32[]{:S(2)}) async-start(), calls=%async_computation.6 | async-start | bytes 10948608 | tf_op jit(solution)/shard_map/all_gather | solution.py:764
  11.8 76.8 %all-to-all-start = ((f32[32,8,128]{2,1,0:T(8,128)}), f32[32,8,128]{2,1,0:T(8,128)S(1)}, u32[]{:S(2)}, u32[]{:S(2)}) async-start(f32[32,8,128]{2,1,0:T(8,128)} %broadcast_in_dim.59), calls=%async_computation | async-start | bytes 262144 | tf_op jit(solution)/shard_map/all_to_all | solution.py:694
  22.2 47.2 %copy-start.49 = (s32[4]{0:T(128)S(1)}, s32[4]{0:T(128)}, u32[]{:S(2)}) copy-start(s32[4]{0:T(128)} %param.33) | copy-start | bytes 52
  22.2 47.8 %copy-start.52 = (pred[24]{0:T(512)(128)(4,1)S(1)}, pred[24]{0:T(512)(128)(4,1)}, u32[]{:S(2)}) copy-start(pred[24]{0:T(512)(128)(4,1)} %constant.319) | copy-start | bytes 76
  22.2 47.8 %copy-start.53 = (pred[24]{0:T(512)(128)(4,1)S(1)}, pred[24]{0:T(512)(128)(4,1)}, u32[]{:S(2)}) copy-start(pred[24]{0:T(512)(128)(4,1)} %constant.320) | copy-start | bytes 76
  22.2 47.8 %copy-start.54 = (pred[24]{0:T(512)(128)(4,1)S(1)}, pred[24]{0:T(512)(128)(4,1)}, u32[]{:S(2)}) copy-start(pred[24]{0:T(512)(128)(4,1)} %constant.321) | copy-start | bytes 76
  22.2 50.4 %copy-start.51 = (s32[24]{0:T(128)S(1)}, s32[24]{0:T(128)}, u32[]{:S(2)}) copy-start(s32[24]{0:T(128)} %param.32) | copy-start | bytes 292
  22.2 55.6 %copy-start.55 = (s32[24]{0:T(128)S(1)}, s32[24]{0:T(128)}, u32[]{:S(2)}) copy-start(s32[24]{0:T(128)} %param.31) | copy-start | bytes 292
  81.0 84.0 %copy-start.1 = (bf16[1000,1024]{1,0:T(8,128)(2,1)}, bf16[1000,1024]{1,0:T(8,128)(2,1)S(1)}, u32[]{:S(2)}) copy-start(bf16[1000,1024]{1,0:T(8,128)(2,1)S(1)} %bitcast_convert_fusion.read_ref) | copy-start | bytes 6144004
  83.9 81.2 %copy-start.5 = (bf16[384,1024]{1,0:T(8,128)(2,1)}, bf16[384,1024]{1,0:T(8,128)(2,1)S(1)}, u32[]{:S(2)}) copy-start(bf16[384,1024]{1,0:T(8,128)(2,1)S(1)} %convert_element_type.485.rff_ref) | copy-start | bytes 2359300
  167.6 8.1 %all-to-all-start.1 = ((f32[4,24,384]{2,1,0:T(8,128)}), f32[4,24,384]{2,1,0:T(8,128)S(1)}, u32[]{:S(2)}, u32[]{:S(2)}) async-start(f32[4,24,384]{2,1,0:T(8,128)} %bitcast.224), calls=%async_computation.1 | async-start | bytes 294912 | tf_op jit(solution)/shard_map/all_to_all | solution.py:793
  171.0 116.6 %all-gather.10.cloned.1.call-start = ((), (), s32[]{:S(2)}) async-start(), calls=%async_computation.7 | async-start | bytes 2230272 | tf_op jit(solution)/shard_map/all_gather | solution.py:797
  191.5 18.7 %collective-permute-start = (bf16[8,288,384]{2,1,0:T(8,128)(2,1)}, bf16[8,288,384]{2,1,0:T(8,128)(2,1)S(1)}, u32[]{:S(2)}, u32[]{:S(2)}) collective-permute-start(bf16[8,288,384]{2,1,0:T(8,128)(2,1)} %get-tuple-element.136), channel_id=1, source_target_pairs={{0,1},{1,0},{2,3},{3,2},{4,5},{5,4},{6,7},{7,6},{8,9},{9,8},{10,11... | collective-permute-start | bytes 5308424 | tf_op jit(solution)/shard_map/ppermute | solution.py:638
  193.5 16.7 %copy-start.17 = (bf16[8,288,384]{2,1,0:T(8,128)(2,1)S(1)}, bf16[8,288,384]{2,1,0:T(8,128)(2,1)}, u32[]{:S(2)}) copy-start(bf16[8,288,384]{2,1,0:T(8,128)(2,1)} %get-tuple-element.143) | copy-start | bytes 5308420
  210.4 23.1 %collective-permute-start.1 = (bf16[8,144,384]{2,1,0:T(8,128)(2,1)S(1)}, bf16[8,144,384]{2,1,0:T(8,128)(2,1)}, u32[]{:S(2)}, u32[]{:S(2)}) collective-permute-start(bf16[8,144,384]{2,1,0:T(8,128)(2,1)S(1)} %add_convert_fusion), channel_id=1, source_target_pairs={{0,2},{2,0},{1,3},{3,1},{4,6},{6,4},{5,7},{7,5},{8,10},{10,8},{9,1... | collective-permute-start | bytes 2654216 | tf_op jit(solution)/shard_map/ppermute | solution.py:638
  210.8 22.8 %collective-permute-start.2 = (bf16[6,288,384]{2,1,0:T(8,128)(2,1)}, bf16[6,288,384]{2,1,0:T(8,128)(2,1)S(1)}, u32[]{:S(2)}, u32[]{:S(2)}) collective-permute-start(bf16[6,288,384]{2,1,0:T(8,128)(2,1)} %get-tuple-element.145), channel_id=1, source_target_pairs={{0,1},{1,0},{2,3},{3,2},{4,5},{5,4},{6,7},{7,6},{8,9},{9,8},{10,11... | collective-permute-start | bytes 3981320 | tf_op jit(solution)/shard_map/ppermute | solution.py:638
  211.0 18.6 %copy-start.21 = (bf16[6,288,384]{2,1,0:T(8,128)(2,1)S(1)}, bf16[6,288,384]{2,1,0:T(8,128)(2,1)}, u32[]{:S(2)}) copy-start(bf16[6,288,384]{2,1,0:T(8,128)(2,1)} %get-tuple-element.155) | copy-start | bytes 3981316
  234.8 19.6 %collective-permute-start.3 = (bf16[4,1,144,384]{3,2,0,1:T(8,128)(2,1)S(1)}, bf16[4,1,144,384]{3,2,0,1:T(8,128)(2,1)S(1)}, u32[]{:S(2)}, u32[]{:S(2)}) collective-permute-start(bf16[4,1,144,384]{3,2,0,1:T(8,128)(2,1)S(1)} %add_convert_fusion.3), channel_id=1, source_target_pairs={{0,4},{4,0},{1,5},{5,1},{2,6},{6,2},{3,7},{7,3},{8,12},{12,8},{9,1... | collective-permute-start | bytes 1327112 | tf_op jit(solution)/shard_map/ppermute | solution.py:638
  236.4 18.0 %collective-permute-start.4 = (bf16[6,144,384]{2,1,0:T(8,128)(2,1)S(1)}, bf16[6,144,384]{2,1,0:T(8,128)(2,1)S(1)}, u32[]{:S(2)}, u32[]{:S(2)}) collective-permute-start(bf16[6,144,384]{2,1,0:T(8,128)(2,1)S(1)} %add_convert_fusion.2), channel_id=1, source_target_pairs={{0,2},{2,0},{1,3},{3,1},{4,6},{6,4},{5,7},{7,5},{8,10},{10,8},{9,1... | collective-permute-start | bytes 1990664 | tf_op jit(solution)/shard_map/ppermute | solution.py:638
  237.0 17.4 %collective-permute-start.5 = (bf16[2,288,384]{2,1,0:T(8,128)(2,1)}, bf16[2,288,384]{2,1,0:T(8,128)(2,1)S(1)}, u32[]{:S(2)}, u32[]{:S(2)}) collective-permute-start(bf16[2,288,384]{2,1,0:T(8,128)(2,1)} %get-tuple-element.157), channel_id=1, source_target_pairs={{0,1},{1,0},{2,3},{3,2},{4,5},{5,4},{6,7},{7,6},{8,9},{9,8},{10,11... | collective-permute-start | bytes 1327112 | tf_op jit(solution)/shard_map/ppermute | solution.py:638
  257.2 71.1 %all-to-all-start.4 = ((bf16[4,144,384]{2,1,0:T(8,128)(2,1)}), bf16[4,144,384]{2,1,0:T(8,128)(2,1)S(1)}, u32[]{:S(2)}, u32[]{:S(2)}) async-start(bf16[4,144,384]{2,1,0:T(8,128)(2,1)} %fusion.5), calls=%async_computation.4 | async-start | bytes 884736 | tf_op jit(solution)/shard_map/all_to_all | solution.py:677
  263.3 22.4 %collective-permute-start.6 = (bf16[3,1,144,384]{3,2,0,1:T(8,128)(2,1)S(1)}, bf16[3,1,144,384]{3,2,0,1:T(8,128)(2,1)S(1)}, u32[]{:S(2)}, u32[]{:S(2)}) collective-permute-start(bf16[3,1,144,384]{3,2,0,1:T(8,128)(2,1)S(1)} %add_convert_fusion.5), channel_id=1, source_target_pairs={{0,4},{4,0},{1,5},{5,1},{2,6},{6,2},{3,7},{7,3},{8,12},{12,8},{9,1... | collective-permute-start | bytes 995336 | tf_op jit(solution)/shard_map/ppermute | solution.py:638
  264.1 21.6 %collective-permute-start.7 = (bf16[2,144,384]{2,1,0:T(8,128)(2,1)S(1)}, bf16[2,144,384]{2,1,0:T(8,128)(2,1)S(1)}, u32[]{:S(2)}, u32[]{:S(2)}) collective-permute-start(bf16[2,144,384]{2,1,0:T(8,128)(2,1)S(1)} %add_convert_fusion.7), channel_id=1, source_target_pairs={{0,2},{2,0},{1,3},{3,1},{4,6},{6,4},{5,7},{7,5},{8,10},{10,8},{9,1... | collective-permute-start | bytes 663560 | tf_op jit(solution)/shard_map/ppermute | solution.py:638
  265.8 20.0 %collective-permute-start.8 = (bf16[6,288,384]{2,1,0:T(8,128)(2,1)}, bf16[6,288,384]{2,1,0:T(8,128)(2,1)S(1)}, u32[]{:S(2)}, u32[]{:S(2)}) collective-permute-start(bf16[6,288,384]{2,1,0:T(8,128)(2,1)} %get-tuple-element.172), channel_id=1, source_target_pairs={{0,1},{1,0},{2,3},{3,2},{4,5},{5,4},{6,7},{7,6},{8,9},{9,8},{10,11... | collective-permute-start | bytes 3981320 | tf_op jit(solution)/shard_map/ppermute | solution.py:638
  265.8 19.8 %copy-start.18 = (bf16[6,288,384]{2,1,0:T(8,128)(2,1)S(1)}, bf16[6,288,384]{2,1,0:T(8,128)(2,1)}, u32[]{:S(2)}) copy-start(bf16[6,288,384]{2,1,0:T(8,128)(2,1)} %get-tuple-element.174) | copy-start | bytes 3981316
  285.7 19.2 %copy-start.36 = (bf16[2,144,384]{2,1,0:T(8,128)(2,1)}, bf16[2,144,384]{2,1,0:T(8,128)(2,1)S(1)}, u32[]{:S(2)}) copy-start(bf16[2,144,384]{2,1,0:T(8,128)(2,1)S(1)} %collective-permute-done.7) | copy-start | bytes 663556
  287.1 24.7 %collective-permute-start.10 = (bf16[6,144,384]{2,1,0:T(8,128)(2,1)}, bf16[6,144,384]{2,1,0:T(8,128)(2,1)}, u32[]{:S(2)}, u32[]{:S(2)}) collective-permute-start(bf16[6,144,384]{2,1,0:T(8,128)(2,1)} %add_convert_fusion.1), channel_id=1, source_target_pairs={{0,2},{2,0},{1,3},{3,1},{4,6},{6,4},{5,7},{7,5},{8,10},{10,8},{9,1... | collective-permute-start | bytes 1990664 | tf_op jit(solution)/shard_map/ppermute | solution.py:638
  287.6 17.9 %copy-start.20 = (bf16[6,288,384]{2,1,0:T(8,128)(2,1)S(1)}, bf16[6,288,384]{2,1,0:T(8,128)(2,1)}, u32[]{:S(2)}) copy-start(bf16[6,288,384]{2,1,0:T(8,128)(2,1)} %copy-done.19) | copy-start | bytes 3981316
  287.6 18.0 %copy-start.29 = (bf16[2,288,384]{2,1,0:T(8,128)(2,1)S(1)}, bf16[2,288,384]{2,1,0:T(8,128)(2,1)}, u32[]{:S(2)}) copy-start(bf16[2,288,384]{2,1,0:T(8,128)(2,1)} %copy-done.27) | copy-start | bytes 1327108
  287.6 20.5 %copy-start.25 = (bf16[6,144,384]{2,1,0:T(8,128)(2,1)S(1)}, bf16[6,144,384]{2,1,0:T(8,128)(2,1)}, u32[]{:S(2)}) copy-start(bf16[6,144,384]{2,1,0:T(8,128)(2,1)} %copy-done.24) | copy-start | bytes 1990660
  287.6 20.5 %copy-start.34 = (bf16[3,1,144,384]{3,2,0,1:T(8,128)(2,1)S(1)}, bf16[3,1,144,384]{3,2,0,1:T(8,128)(2,1)}, u32[]{:S(2)}) copy-start(bf16[3,1,144,384]{3,2,0,1:T(8,128)(2,1)} %copy-done.33) | copy-start | bytes 995332
  304.9 6.9 %collective-permute-start.11 = (bf16[8,48,512]{2,1,0:T(8,128)(2,1)}, bf16[8,48,512]{2,1,0:T(8,128)(2,1)S(1)}, u32[]{:S(2)}, u32[]{:S(2)}) collective-permute-start(bf16[8,48,512]{2,1,0:T(8,128)(2,1)} %bitcast.36), channel_id=1, source_target_pairs={{0,1},{1,0},{2,3},{3,2},{4,5},{5,4},{6,7},{7,6},{8,9},{9,8},{10,11... | collective-permute-start | bytes 1179656 | tf_op jit(solution)/shard_map/ppermute | solution.py:638
  305.2 6.6 %collective-permute-start.12 = (bf16[2,288,384]{2,1,0:T(8,128)(2,1)}, bf16[2,288,384]{2,1,0:T(8,128)(2,1)S(1)}, u32[]{:S(2)}, u32[]{:S(2)}) collective-permute-start(bf16[2,288,384]{2,1,0:T(8,128)(2,1)} %get-tuple-element.177), channel_id=1, source_target_pairs={{0,1},{1,0},{2,3},{3,2},{4,5},{5,4},{6,7},{7,6},{8,9},{9,8},{10,11... | collective-permute-start | bytes 1327112 | tf_op jit(solution)/shard_map/ppermute | solution.py:638
  306.6 5.2 %collective-permute-start.9 = (bf16[1,1,144,384]{3,2,1,0:T(8,128)(2,1)S(1)}, bf16[1,1,144,384]{3,2,1,0:T(8,128)(2,1)S(1)}, u32[]{:S(2)}, u32[]{:S(2)}) collective-permute-start(bf16[1,1,144,384]{3,2,1,0:T(8,128)(2,1)S(1)} %fusion.16), channel_id=1, source_target_pairs={{0,4},{4,0},{1,5},{5,1},{2,6},{6,2},{3,7},{7,3},{8,12},{12,8},{9,1... | collective-permute-start | bytes 331784 | tf_op jit(solution)/shard_map/ppermute | solution.py:638
  311.8 14.9 %copy-start.31 = (bf16[2,288,384]{2,1,0:T(8,128)(2,1)}, bf16[2,288,384]{2,1,0:T(8,128)(2,1)S(1)}, u32[]{:S(2)}) copy-start(bf16[2,288,384]{2,1,0:T(8,128)(2,1)S(1)} %collective-permute-done.12) | copy-start | bytes 1327108
  313.1 12.3 %collective-permute-start.13 = (bf16[3,1,144,384]{3,2,0,1:T(8,128)(2,1)S(1)}, bf16[3,1,144,384]{3,2,0,1:T(8,128)(2,1)S(1)}, u32[]{:S(2)}, u32[]{:S(2)}) collective-permute-start(bf16[3,1,144,384]{3,2,0,1:T(8,128)(2,1)S(1)} %add_convert_fusion.4), channel_id=1, source_target_pairs={{0,4},{4,0},{1,5},{5,1},{2,6},{6,2},{3,7},{7,3},{8,12},{12,8},{9,1... | collective-permute-start | bytes 995336 | tf_op jit(solution)/shard_map/ppermute | solution.py:638
  314.6 7.9 %collective-permute-start.14 = (bf16[8,48,256]{2,1,0:T(8,128)(2,1)S(1)}, bf16[8,48,256]{2,1,0:T(8,128)(2,1)S(1)}, u32[]{:S(2)}, u32[]{:S(2)}) collective-permute-start(bf16[8,48,256]{2,1,0:T(8,128)(2,1)S(1)} %add_convert_fusion.8), channel_id=1, source_target_pairs={{0,2},{2,0},{1,3},{3,1},{4,6},{6,4},{5,7},{7,5},{8,10},{10,8},{9,1... | collective-permute-start | bytes 589832 | tf_op jit(solution)/shard_map/ppermute | solution.py:638
  316.3 9.0 %collective-permute-start.15 = (bf16[2,144,384]{2,1,0:T(8,128)(2,1)S(1)}, bf16[2,144,384]{2,1,0:T(8,128)(2,1)S(1)}, u32[]{:S(2)}, u32[]{:S(2)}) collective-permute-start(bf16[2,144,384]{2,1,0:T(8,128)(2,1)S(1)} %add_convert_fusion.6), channel_id=1, source_target_pairs={{0,2},{2,0},{1,3},{3,1},{4,6},{6,4},{5,7},{7,5},{8,10},{10,8},{9,1... | collective-permute-start | bytes 663560 | tf_op jit(solution)/shard_map/ppermute | solution.py:638
  326.1 8.7 %collective-permute-start.16 = (bf16[4,1,48,256]{3,2,0,1:T(8,128)(2,1)}, bf16[4,1,48,256]{3,2,0,1:T(8,128)(2,1)S(1)}, u32[]{:S(2)}, u32[]{:S(2)}) collective-permute-start(bf16[4,1,48,256]{3,2,0,1:T(8,128)(2,1)} %add_convert_fusion.13), channel_id=1, source_target_pairs={{0,4},{4,0},{1,5},{5,1},{2,6},{6,2},{3,7},{7,3},{8,12},{12,8},{9,1... | collective-permute-start | bytes 294920 | tf_op jit(solution)/shard_map/ppermute | solution.py:638
  326.8 8.0 %collective-permute-start.17 = (bf16[1,1,144,384]{3,2,1,0:T(8,128)(2,1)S(1)}, bf16[1,1,144,384]{3,2,1,0:T(8,128)(2,1)S(1)}, u32[]{:S(2)}, u32[]{:S(2)}) collective-permute-start(bf16[1,1,144,384]{3,2,1,0:T(8,128)(2,1)S(1)} %fusion.17), channel_id=1, source_target_pairs={{0,4},{4,0},{1,5},{5,1},{2,6},{6,2},{3,7},{7,3},{8,12},{12,8},{9,1... | collective-permute-start | bytes 331784 | tf_op jit(solution)/shard_map/ppermute | solution.py:638
  328.3 15.8 %all-to-all-start.3 = ((bf16[4,144,384]{2,1,0:T(8,128)(2,1)}), bf16[4,144,384]{2,1,0:T(8,128)(2,1)S(1)}, u32[]{:S(2)}, u32[]{:S(2)}) async-start(bf16[4,144,384]{2,1,0:T(8,128)(2,1)} %pad_maximum_fusion.2), calls=%async_computation.3 | async-start | bytes 884736 | tf_op jit(solution)/shard_map/all_to_all | solution.py:677
  344.1 16.3 %all-to-all-start.2 = ((bf16[4,176,384]{2,1,0:T(8,128)(2,1)}), bf16[4,176,384]{2,1,0:T(8,128)(2,1)S(1)}, u32[]{:S(2)}, u32[]{:S(2)}) async-start(bf16[4,176,384]{2,1,0:T(8,128)(2,1)} %pad_maximum_fusion.1), calls=%async_computation.2 | async-start | bytes 1081344 | tf_op jit(solution)/shard_map/all_to_all | solution.py:677
  347.6 17.9 %copy-start.23 = (f32[965,48]{0,1:T(8,128)S(1)}, f32[965,48]{0,1:T(8,128)}, u32[]{:S(2)}) copy-start(f32[965,48]{0,1:T(8,128)} %param.34) | copy-start | bytes 555844
  348.3 18.2 %copy-start.40 = (f32[965,48]{0,1:T(8,128)S(1)}, f32[965,48]{0,1:T(8,128)}, u32[]{:S(2)}) copy-start(f32[965,48]{0,1:T(8,128)} %param.35) | copy-start | bytes 555844
  351.0 16.5 %copy-start.41 = (f32[965,48]{0,1:T(8,128)S(1)}, f32[965,48]{0,1:T(8,128)}, u32[]{:S(2)}) copy-start(f32[965,48]{0,1:T(8,128)} %param.36) | copy-start | bytes 555844
  351.0 17.4 %copy-start.42 = (f32[965,48]{0,1:T(8,128)S(1)}, f32[965,48]{0,1:T(8,128)}, u32[]{:S(2)}) copy-start(f32[965,48]{0,1:T(8,128)} %param.37) | copy-start | bytes 555844
  362.5 11.1 %all-to-all-start.5 = ((f32[32,8,128]{2,1,0:T(8,128)}), f32[32,8,128]{2,1,0:T(8,128)S(1)}, u32[]{:S(2)}, u32[]{:S(2)}) async-start(f32[32,8,128]{2,1,0:T(8,128)} %broadcast_in_dim.70), calls=%async_computation.5 | async-start | bytes 262144 | tf_op jit(solution)/shard_map/all_to_all | solution.py:694
  365.4 33.3 %all-gather.12.cloned.1.call-start = ((), (), s32[]{:S(2)}) async-start(), calls=%async_computation.8 | async-start | bytes 1781760 | tf_op jit(solution)/shard_map/all_gather | solution.py:681
  (35 other events, 171.4 us)
Sparse Core Ops, SparseCore 0:
  11.5 92.0 all-gather.7
  192.4 57.6 all-gather.9
  371.0 20.0 all-gather.11
